TPU v7x, 32 devices: a whole 2x2x4 slice. The times are simulated.
32 devices in a mesh: group: 2 (over y), tile: 16 (over z, x, core).
Axes of the slice: x: 2, y: 2, z: 4, core: 2. Of those that a mesh axis runs over, the one named last changes fastest.
Arguments:
- site_tensors: bfloat16 [16, 6, 2, 65536], P('tile', 'group'), may hold values from -6 to 6
- msg_in: float32 [16, 6, 4, 256], P('tile', 'group'), may hold values from -6 to 6
Outputs:
- new_tensors: bfloat16 [16, 6, 2, 65536], P('tile', 'group')
- messages: float32 [16, 6, 4, 256], P('tile', 'group')
All inputs are finite; a program needn't handle non-finite values.
Results may differ from a plain program's by a relative error of at most 0.029.
The roundings to bfloat16 on the way count: a program that leaves them out, or rounds other values in their place, can miss the bound.
Values may be sent and summed in bfloat16 or wider, within the bound.
A program may use at most 256 MiB of HBM per device.

v0:
```python
import functools
import math

import jax
import jax.numpy as jnp
from jax import lax
from jax.experimental import pallas as pl
from jax.experimental.pallas import tpu as pltpu
from jax.sharding import PartitionSpec as P

ITERS = 2
NS_STEPS = 6
LANES = 128
EPSILON = 1e-06
COUPLING = 0.5
FIELD = 0.3
F32 = jnp.float32
BF16 = jnp.bfloat16
MESH = pl.DeviceIdType.MESH


def iota(shape, axis):
    return lax.broadcasted_iota(jnp.int32, shape, axis)


def dot(a, b):
    return jnp.dot(a, b, preferred_element_type=F32)


def dot_nt(a, b):
    return lax.dot_general(a, b, (((1,), (1,)), ((), ())), preferred_element_type=F32)


def dot_tn(a, b):
    return lax.dot_general(a, b, (((0,), (0,)), ((), ())), preferred_element_type=F32)


def parts(value, count):
    out = []
    for _ in range(count):
        piece = value.astype(BF16)
        out.append(piece)
        value = value - piece.astype(F32)
    return out


def select_dot(value, selector, count):
    total = None
    for piece in parts(value, count):
        term = dot(piece, selector)
        total = term if total is None else total + term
    return total


def one_hot(mask):
    return jnp.where(mask, 1.0, 0.0).astype(BF16)


def build_kron(kron_ref, slot, first, second):
    D = first.shape[0]
    for d in range(D):
        kron_ref[slot, d * D : (d + 1) * D, :] = (first[d : d + 1, :] * second).astype(BF16)


def permutation(DD, rows, mixed, out_axis):
    p, k = iota((DD, DD), out_axis), iota((DD, DD), 1 - out_axis)
    row_bits = rows.bit_length() - 1
    return one_hot(k == (p & (rows - 1)) * mixed + (p >> row_bits))


def messages_kernel(tiles, groups, cols, D, a_ref, msg_ref, ax_ref, env_ref, mout_ref,
           x_ref, xt_ref, kron_ref, gram_ref,
           send_up, send_down, send_side, recv_up, recv_down, recv_side,
           send_sem, recv_sem):
    tile = lax.axis_index("tile")
    group = lax.axis_index("group")
    DD = D * D
    shift = D.bit_length() - 1
    halves = DD // LANES
    mixed = 2 * halves
    rows = DD // mixed
    legs = 4 * cols
    wide = legs * D
    has_up = tile > 0
    has_down = tile < tiles - 1

    barrier = pltpu.get_barrier_semaphore()

    @pl.when(has_up)
    def _():
        pl.semaphore_signal(barrier, inc=1, device_id={"tile": tile - 1}, device_id_type=MESH)

    @pl.when(has_down)
    def _():
        pl.semaphore_signal(barrier, inc=1, device_id={"tile": tile + 1}, device_id_type=MESH)

    pl.semaphore_signal(barrier, inc=1, device_id={"group": 1 - group}, device_id_type=MESH)

    lane = iota((D, DD), 1)
    row = iota((D, DD), 0)
    major = one_hot((lane >> shift) == row)
    minor = one_hot((lane & (D - 1)) == row)
    both = jnp.concatenate([major, minor], axis=1)
    major_t = one_hot((iota((DD, D), 0) >> shift) == iota((DD, D), 1))
    minor_t = one_hot((iota((DD, D), 0) & (D - 1)) == iota((DD, D), 1))

    unfold_mask = (lane >> shift) == row
    flat = msg_ref[...].reshape(legs, DD)
    spread = jnp.concatenate(
        [jnp.where(unfold_mask, flat[m : m + 1, :], 0.0) for m in range(legs)], axis=0
    )
    edge_all = select_dot(spread, minor_t, 3)
    edge = [edge_all[m * D : (m + 1) * D] for m in range(legs)]

    gather = permutation(DD, rows, mixed, 0)

    def unmix(i):
        for b in range(0, mixed, 2):
            pair = jnp.concatenate(
                [a_ref[i, b * DD : (b + 1) * DD, :], a_ref[i, (b + 1) * DD : (b + 2) * DD, :]],
                axis=1,
            )
            block = dot(gather, pair).astype(BF16)
            for c in range(2):
                for g in range(mixed):
                    x_ref[
                        i,
                        g % 2,
                        (b + c) * rows : (b + c + 1) * rows,
                        (g // 2) * LANES : (g // 2 + 1) * LANES,
                    ] = block[g * rows : (g + 1) * rows, c * LANES : (c + 1) * LANES]
        for s in range(2):
            xt_ref[i, s] = x_ref[i, s].T

    def reduce_major(gram, weight):
        total = gram[:D] * weight[0:1, :]
        for d in range(1, D):
            total = total + gram[d * D : (d + 1) * D] * weight[d : d + 1, :]
        return total

    def reduce_minor(gram, weight):
        return jnp.concatenate(
            [
                jnp.sum(gram[d * D : (d + 1) * D] * weight, axis=0, keepdims=True)
                for d in range(D)
            ],
            axis=0,
        )

    def kinds_of(totals):
        if len(totals) == 1:
            return totals
        return [totals[0] + totals[1], totals[0] - totals[1]]

    def outgoing(turn, incoming, last):
        stacked = jnp.concatenate([v.astype(BF16) for v in incoming], axis=0)
        spread = dot(stacked, both)
        kinds = 2 if last else 1

        def by_major(m):
            return spread[m * D : (m + 1) * D, :DD]

        def by_minor(m):
            return spread[m * D : (m + 1) * D, DD:]

        def normalised(totals, selector, slots):
            blocks = []
            for kind in range(kinds):
                rows_of = jnp.concatenate([t[kind] for t in totals], axis=0)
                blocks.append(select_dot(rows_of, selector, 2))
            out = {}
            for n, slot in enumerate(slots):
                own = [b[n * D : (n + 1) * D] for b in blocks]
                power = jnp.sum(own[0] * own[0], axis=(0, 1), keepdims=True) / DD
                scale = jnp.sqrt(power + EPSILON)
                out[slot] = [v / scale for v in own]
            return out

        firsts = []
        for i in range(cols):
            if turn == 0:
                unmix(i)
            for path in range(2):
                left, right = (x_ref, xt_ref) if path == 0 else (xt_ref, x_ref)
                far = i * 4 + 2 * (1 - path)
                near = i * 4 + 2 * path
                slot = i * 2 + path
                build_kron(kron_ref, slot, by_major(far), by_minor(far + 1))
                y = [dot(left[i, s], kron_ref[slot]).astype(BF16) for s in range(2)]
                if last:
                    grams = [dot(y[s], right[i, s]) for s in range(2)]
                else:
                    grams = [dot(y[0], right[i, 0]) + dot(y[1], right[i, 1])]
                for k, gram in enumerate(grams):
                    gram_ref[slot, k] = gram
                firsts.append(kinds_of([reduce_minor(g, by_minor(near + 1)) for g in grams]))

        def seconds(slots):
            totals = []
            for slot in slots:
                weight = by_major((slot // 2) * 4 + 2 * (slot % 2))
                totals.append(
                    kinds_of([reduce_major(gram_ref[slot, k], weight) for k in range(kinds)])
                )
            return normalised(totals, minor_t, slots)

        vertical = normalised(firsts, major_t, list(range(2 * cols)))
        ends = [0, 2 * cols - 1]
        sides = seconds(ends)

        def rest():
            others = [slot for slot in range(2 * cols) if slot not in ends]
            if others:
                sides.update(seconds(others))
            values = []
            for kind in range(kinds):
                blocks = []
                for slot in range(2 * cols):
                    blocks += [vertical[slot][kind], sides[slot][kind]]
                values.append(blocks)
            return values

        return vertical, sides, rest

    def exchange(turn, vertical, sides, kinds):
        width = kinds * cols * D

        def packed(path):
            return jnp.concatenate(
                [vertical[2 * i + path][k] for k in range(kinds) for i in range(cols)], axis=1
            )

        up_src = send_up.at[turn]
        down_src = send_down.at[turn]
        side_src = send_side.at[turn]
        send_up[turn, :, :width] = packed(0)
        send_down[turn, :, :width] = packed(1)
        side_right = jnp.concatenate(sides[2 * cols - 1], axis=1)
        side_left = jnp.concatenate(sides[0], axis=1)
        send_side[turn, :, : kinds * D] = jnp.where(group == 0, side_right, side_left)

        def copy(src, dst, k, device):
            return pltpu.make_async_remote_copy(
                src_ref=src, dst_ref=dst.at[turn], send_sem=send_sem.at[turn, k],
                recv_sem=recv_sem.at[turn, k], device_id=device, device_id_type=MESH,
            )

        to_up = copy(up_src, recv_down, 0, {"tile": tile - 1})
        to_down = copy(down_src, recv_up, 1, {"tile": tile + 1})
        to_side = copy(side_src, recv_side, 2, {"group": 1 - group})

        @pl.when(has_up)
        def _():
            to_up.start()

        @pl.when(has_down)
        def _():
            to_down.start()

        to_side.start()
        return to_up, to_down, to_side

    def finish(turn, copies, values):
        to_up, to_down, to_side = copies
        kinds = len(values)
        width = kinds * cols * D

        def border(leg):
            blocks = [edge[i * 4 + leg] for i in range(cols)]
            if kinds == 2:
                blocks += [jnp.zeros((D, D), F32)] * cols
            return jnp.concatenate(blocks, axis=1)

        @pl.when(has_up)
        def _():
            to_up.wait_send()
            to_down.wait_recv()

        @pl.when(jnp.logical_not(has_up))
        def _():
            recv_up[turn, :, :width] = border(0)

        @pl.when(has_down)
        def _():
            to_down.wait_send()
            to_up.wait_recv()

        @pl.when(jnp.logical_not(has_down))
        def _():
            recv_down[turn, :, :width] = border(2)

        to_side.wait()
        from_up, from_down, from_side = recv_up[turn], recv_down[turn], recv_side[turn]
        routed = []
        for kind in range(kinds):
            blocks = []
            for i in range(cols):
                at = (kind * cols + i) * D
                side = from_side[:, kind * D : (kind + 1) * D]
                zero = jnp.zeros((D, D), F32)
                out_left = edge[i * 4 + 1] if kind == 0 else zero
                out_right = edge[i * 4 + 3] if kind == 0 else zero
                blocks.append(from_up[:, at : at + D])
                if i > 0:
                    blocks.append(values[kind][(i - 1) * 4 + 3])
                else:
                    blocks.append(jnp.where(group == 0, out_left, side))
                blocks.append(from_down[:, at : at + D])
                if i < cols - 1:
                    blocks.append(values[kind][(i + 1) * 4 + 1])
                else:
                    blocks.append(jnp.where(group == groups - 1, out_right, side))
            routed.append(blocks)
        return routed

    incoming = edge
    for turn in range(ITERS):
        last = turn == ITERS - 1
        vertical, sides, rest = outgoing(turn, incoming, last)
        if turn == 0:
            inside = jnp.logical_and(has_up, has_down)

            @pl.when(inside)
            def _():
                pl.semaphore_wait(barrier, 3)

            @pl.when(jnp.logical_not(inside))
            def _():
                pl.semaphore_wait(barrier, 2)

        copies = exchange(turn, vertical, sides, 2 if last else 1)
        values = rest()
        if turn == 0:
            for i in range(cols):
                a0, a1 = x_ref[i, 0].astype(F32), x_ref[i, 1].astype(F32)
                ch, sh = math.cosh(FIELD), math.sinh(FIELD)
                ax_ref[i, 0] = (ch * a0 + sh * a1).astype(BF16)
                ax_ref[i, 1] = (ch * a1 + sh * a0).astype(BF16)
        routed = finish(turn, copies, values)
        incoming = routed[0]

    mout_ref[...] = jnp.concatenate(incoming, axis=0)
    env_ref[0] = jnp.concatenate([o + n for o, n in zip(values[0], routed[0])], axis=1)
    env_ref[1] = jnp.concatenate([o + n for o, n in zip(values[1], routed[1])], axis=1)
    lane_w = iota((D, wide), 1)
    leg_of = (lane_w >> shift) & 3
    col_of = (lane_w >> (shift + 2)) + group * cols
    at_edge = (
        ((leg_of == 0) & (tile == 0))
        | ((leg_of == 2) & (tile == tiles - 1))
        | ((leg_of == 1) & (col_of == 0))
        | ((leg_of == 3) & (col_of == groups * cols - 1))
    )
    env_ref[2] = jnp.where(at_edge, 1.0, 0.0).astype(F32)


def gates_kernel(cols, D, ax_ref, env_ref, in_ref, out_hbm, mout_hbm,
                 kron_ref, out_ref, mout_ref, store_sem):
    DD = D * D
    shift = D.bit_length() - 1
    mixed = 2 * (DD // LANES)
    rows = DD // mixed
    legs = 4 * cols
    wide = legs * D
    lane = iota((D, DD), 1)
    row = iota((D, DD), 0)
    major = one_hot((lane >> shift) == row)
    minor = one_hot((lane & (D - 1)) == row)
    both = jnp.concatenate([major, minor], axis=1)

    spread = select_dot(in_ref[...], minor, 3)
    unfold_mask = (lane >> shift) == row
    flat_rows = [
        jnp.sum(
            jnp.where(unfold_mask, spread[m * D : (m + 1) * D], 0.0), axis=0, keepdims=True
        )
        for m in range(legs)
    ]
    mout_ref[...] = jnp.concatenate(flat_rows, axis=0).reshape(cols, 4, DD)
    store_msg = pltpu.make_async_copy(mout_ref, mout_hbm, store_sem.at[cols])
    store_msg.start()

    g0, g1 = math.cosh(COUPLING), math.sinh(COUPLING)
    cross = math.sqrt(g0 * g1)
    root2 = math.sqrt(2.0)
    msg_sum, twist_sum = env_ref[0], env_ref[1]
    y_top = ((g0 * msg_sum + cross * twist_sum) / root2).astype(BF16)
    y_bot = ((cross * twist_sum + g1 * msg_sum) / root2).astype(BF16)
    y_both = jnp.concatenate([y_top, y_bot], axis=0)
    same = (iota((wide, wide), 0) >> shift) == (iota((wide, wide), 1) >> shift)
    same_bf = one_hot(same)
    lane_w = iota((D, wide), 1)
    unit = jnp.where((lane_w & (D - 1)) == iota((D, wide), 0), 1.0, 0.0).astype(F32)

    def diagonal(value):
        return jnp.concatenate([value] * legs, axis=0) * same_bf

    def times(left, right):
        count = left.shape[0]
        (l_hi, l_lo), (r_hi, r_lo) = parts(left, 2), parts(right, 2)
        main = dot(jnp.concatenate([l_hi, l_lo], axis=0), diagonal(r_hi))
        return main[:count] + (main[count:] + dot(l_hi, diagonal(r_lo)))

    full = jnp.where(same, dot_tn(y_both, y_both), 0.0)
    gram = full[:D]
    for m in range(1, legs):
        gram = gram + full[m * D : (m + 1) * D]
    diag = jnp.sum(gram * unit, axis=0, keepdims=True)
    trace = select_dot(jnp.broadcast_to(diag, (8, wide)), same_bf, 3)[0:1] + EPSILON
    current = gram / trace
    factor = 1.5 * unit - 0.5 * current
    inverse = factor
    current = times(current, factor)
    for step in range(1, NS_STEPS):
        factor = 1.5 * unit - 0.5 * times(inverse, current)
        if step < NS_STEPS - 1:
            stepped = times(jnp.concatenate([inverse, current], axis=0), factor)
            inverse, current = stepped[:D], stepped[D:]
        else:
            inverse = times(inverse, factor)
    q_both = dot(y_both, diagonal(inverse.astype(BF16))) / jnp.sqrt(trace)
    first = math.sqrt(g0) * q_both[:D]
    second = math.sqrt(g1) * q_both[D:]
    at_edge = env_ref[2] > 0.5
    scatter = permutation(DD, rows, mixed, 1)
    spreads = []
    for weight in (first + second, first - second):
        weight = jnp.where(at_edge, unit, weight)
        spreads.append(dot(weight.T.astype(BF16), both))
    stores = [
        pltpu.make_async_copy(out_ref.at[i], out_hbm.at[i], store_sem.at[i]) for i in range(cols)
    ]
    def gate(i):
        m = i * 4
        gated = []
        for s in range(2):
            w = spreads[s]
            slot = (i * 2 + s) * 2
            build_kron(
                kron_ref, slot, w[(m + 2) * D : (m + 3) * D, :DD], w[(m + 3) * D : (m + 4) * D, DD:]
            )
            build_kron(
                kron_ref, slot + 1, w[m * D : (m + 1) * D, :DD], w[(m + 1) * D : (m + 2) * D, DD:]
            )
            half = dot_nt(ax_ref[i, s], kron_ref[slot]).astype(BF16)
            gated.append(dot(kron_ref[slot + 1], half).astype(BF16))
        return gated

    def emit(i, gated):
        for b in range(0, mixed, 2):
            block = jnp.concatenate(
                [
                    jnp.concatenate(
                        [
                            gated[g % 2][
                                (b + c) * rows : (b + c + 1) * rows,
                                (g // 2) * LANES : (g // 2 + 1) * LANES,
                            ]
                            for c in range(2)
                        ],
                        axis=1,
                    )
                    for g in range(mixed)
                ],
                axis=0,
            )
            done = dot(scatter, block).astype(BF16)
            for c in range(2):
                out_ref[i, (b + c) * DD : (b + c + 1) * DD, :] = done[
                    :, c * LANES : (c + 1) * LANES
                ]
        stores[i].start()

    waiting = gate(0)
    for i in range(cols):
        following = gate(i + 1) if i + 1 < cols else None
        emit(i, waiting)
        waiting = following
    for store in stores + [store_msg]:
        store.wait()


def per_device(tiles, groups, site_tensors, msg_in):
    _, cols, _, size = site_tensors.shape
    DD = msg_in.shape[-1]
    D = math.isqrt(DD)
    chunks = size // LANES
    a = site_tensors.reshape(cols, 2, chunks, LANES).transpose(0, 2, 1, 3)
    a = a.reshape(cols, 2 * chunks, LANES)
    wide = 2 * cols * D
    legs = 4 * cols
    vmem = pl.BlockSpec(memory_space=pltpu.VMEM)
    hbm = pl.BlockSpec(memory_space=pltpu.HBM)
    gated, env, stacked = pl.pallas_call(
        functools.partial(messages_kernel, tiles, groups, cols, D),
        out_shape=(
            jax.ShapeDtypeStruct((cols, 2, DD, DD), BF16),
            jax.ShapeDtypeStruct((3, D, legs * D), F32),
            jax.ShapeDtypeStruct((legs * D, D), F32),
        ),
        in_specs=[vmem, vmem],
        out_specs=(vmem, vmem, vmem),
        scratch_shapes=[
            pltpu.VMEM((cols, 2, DD, DD), BF16),
            pltpu.VMEM((cols, 2, DD, DD), BF16),
            pltpu.VMEM((2 * cols, DD, DD), BF16),
            pltpu.VMEM((2 * cols, 2, DD, DD), F32),
            pltpu.VMEM((ITERS, D, wide), F32),
            pltpu.VMEM((ITERS, D, wide), F32),
            pltpu.VMEM((ITERS, D, 2 * D), F32),
            pltpu.VMEM((ITERS, D, wide), F32),
            pltpu.VMEM((ITERS, D, wide), F32),
            pltpu.VMEM((ITERS, D, 2 * D), F32),
            pltpu.SemaphoreType.DMA((ITERS, 3)),
            pltpu.SemaphoreType.DMA((ITERS, 3)),
        ],
        compiler_params=pltpu.CompilerParams(
            collective_id=0, has_side_effects=True, vmem_limit_bytes=24 * 2**20
        ),
    )(a, msg_in[0])
    out, messages = pl.pallas_call(
        functools.partial(gates_kernel, cols, D),
        out_shape=(
            jax.ShapeDtypeStruct(a.shape, BF16),
            jax.ShapeDtypeStruct((cols, 4, DD), F32),
        ),
        in_specs=[vmem, vmem, vmem],
        out_specs=(hbm, hbm),
        scratch_shapes=[
            pltpu.VMEM((4 * cols, DD, DD), BF16),
            pltpu.VMEM(a.shape, BF16),
            pltpu.VMEM((cols, 4, DD), F32),
            pltpu.SemaphoreType.DMA((cols + 1,)),
        ],
        compiler_params=pltpu.CompilerParams(vmem_limit_bytes=24 * 2**20),
    )(gated, env, stacked)
    out = out.reshape(cols, chunks, 2, LANES).transpose(0, 2, 1, 3)
    return out.reshape(1, cols, 2, size), messages[None]


def solution(mesh):
    spec = P("tile", "group", None, None)
    return jax.shard_map(
        functools.partial(per_device, mesh.shape["tile"], mesh.shape["group"]),
        mesh=mesh, in_specs=(spec, spec), out_specs=(spec, spec), check_vma=False,
    )
```

profile of v0, /device:TPU:1, one launch (start us, length us, event | category | flops | bytes accessed | tf_op | source)
XLA Modules:
  0.0 19.0 jit_solution(16019051047325696535)
XLA Ops:
  0.6 0.0 copy-start
  0.6 1.1 %copy-done = bf16[1,3,2,65536]{3,2,1,0:T(2,128)(2,1)S(1)} copy-done((bf16[1,3,2,65536]{3,2,1,0:T(2,128)(2,1)S(1)}, bf16[1,3,2,65536]{3,2,1,0:T(2,128)(2,1)}, u32[]{:S(2)}) %copy-start) | copy-done | bytes 786456
  1.8 0.0 copy-start.1
  1.8 0.7 %copy-done.1 = f32[1,3,4,256]{3,2,1,0:T(4,128)S(1)} copy-done((f32[1,3,4,256]{3,2,1,0:T(4,128)S(1)}, f32[1,3,4,256]{3,2,1,0:T(4,128)}, u32[]{:S(2)}) %copy-start.1) | copy-done | bytes 12312
  2.5 11.7 %shard_map.41 = (bf16[3,2,256,256]{3,2,1,0:T(8,128)(2,1)S(1)}, f32[3,16,192]{2,1,0:T(8,128)S(1)}, f32[192,16]{1,0:T(8,128)S(1)}) custom-call(bf16[3,1024,128]{2,1,0:T(8,128)(2,1)S(1)} %bitcast.12, f32[3,4,256]{2,1,0:T(4,128)S(1)} %bitcast.13), custom_call_target="tpu_custom_call" | custom-call | tf_op jit(solution)/shard_map/pallas_call | solution.py:494
  14.2 4.8 %shard_map.42 = (bf16[3,1024,128]{2,1,0:T(8,128)(2,1)}, f32[3,4,256]{2,1,0:T(4,128)}) custom-call(bf16[3,2,256,256]{3,2,1,0:T(8,128)(2,1)S(1)} %get-tuple-element.7.ax_ref, f32[3,16,192]{2,1,0:T(8,128)S(1)} %get-tuple-element.8.env_ref, f32[192,16]{1,0:T(8,128)S(1)} %get-tuple-element.9.in_ref), custom_call_target="tpu_custom_call" | custom-call | tf_op jit(solution)/shard_map/pallas_call | solution.py:521
Async XLA Ops:
  0.6 1.1 %copy-start = (bf16[1,3,2,65536]{3,2,1,0:T(2,128)(2,1)S(1)}, bf16[1,3,2,65536]{3,2,1,0:T(2,128)(2,1)}, u32[]{:S(2)}) copy-start(bf16[1,3,2,65536]{3,2,1,0:T(2,128)(2,1)} %param.2) | copy-start | bytes 2359300
  1.8 0.7 %copy-start.1 = (f32[1,3,4,256]{3,2,1,0:T(4,128)S(1)}, f32[1,3,4,256]{3,2,1,0:T(4,128)}, u32[]{:S(2)}) copy-start(f32[1,3,4,256]{3,2,1,0:T(4,128)} %param.3) | copy-start | bytes 36868
where the time goes:
time: 19.3 us; the launch traced here: 19 us
  Pallas kernels  16.5 us (85%)
  local copies, waits for them, and re-layouts  1.83 us (9%)
  between operations  0.65 us (3%)
    pallas_call x1, Pallas kernels, per_device(): pl.pallas_call(functools.partial(messages_kernel, tiles, groups, cols, D)...  11.7 us
    pallas_call x1, Pallas kernels, per_device(): pl.pallas_call(functools.partial(gates_kernel, cols, D), out_shape=(jax.S...  4.83 us
    unnamed x4, local copies, waits for them, and re-layouts  1.83 us

commit v1 on v0

--- a/solution.py
+++ b/solution.py
@@ -68,10 +68,16 @@
     return one_hot(k == (p & (rows - 1)) * mixed + (p >> row_bits))
 
 
-def messages_kernel(tiles, groups, cols, D, a_ref, msg_ref, ax_ref, env_ref, mout_ref,
-           x_ref, xt_ref, kron_ref, gram_ref,
+def messages_kernel(tiles, groups, cols, D, a_hbm, msg_hbm, ax_ref, env_ref, mout_ref,
+           a_ref, msg_ref, x_ref, xt_ref, kron_ref, gram_ref,
            send_up, send_down, send_side, recv_up, recv_down, recv_side,
-           send_sem, recv_sem):
+           send_sem, recv_sem, load_sem):
+    loads = [pltpu.make_async_copy(msg_hbm, msg_ref, load_sem.at[cols])]
+    loads += [
+        pltpu.make_async_copy(a_hbm.at[i], a_ref.at[i], load_sem.at[i]) for i in range(cols)
+    ]
+    for load in loads:
+        load.start()
     tile = lax.axis_index("tile")
     group = lax.axis_index("group")
     DD = D * D
@@ -105,6 +111,7 @@
     minor_t = one_hot((iota((DD, D), 0) & (D - 1)) == iota((DD, D), 1))
 
     unfold_mask = (lane >> shift) == row
+    loads[0].wait()
     flat = msg_ref[...].reshape(legs, DD)
     spread = jnp.concatenate(
         [jnp.where(unfold_mask, flat[m : m + 1, :], 0.0) for m in range(legs)], axis=0
@@ -179,6 +186,7 @@
         firsts = []
         for i in range(cols):
             if turn == 0:
+                loads[1 + i].wait()
                 unmix(i)
             for path in range(2):
                 left, right = (x_ref, xt_ref) if path == 0 else (xt_ref, x_ref)
@@ -498,9 +506,11 @@
             jax.ShapeDtypeStruct((3, D, legs * D), F32),
             jax.ShapeDtypeStruct((legs * D, D), F32),
         ),
-        in_specs=[vmem, vmem],
+        in_specs=[hbm, hbm],
         out_specs=(vmem, vmem, vmem),
         scratch_shapes=[
+            pltpu.VMEM(a.shape, BF16),
+            pltpu.VMEM((cols, 4, DD), F32),
             pltpu.VMEM((cols, 2, DD, DD), BF16),
             pltpu.VMEM((cols, 2, DD, DD), BF16),
             pltpu.VMEM((2 * cols, DD, DD), BF16),
@@ -513,6 +523,7 @@
             pltpu.VMEM((ITERS, D, 2 * D), F32),
             pltpu.SemaphoreType.DMA((ITERS, 3)),
             pltpu.SemaphoreType.DMA((ITERS, 3)),
+            pltpu.SemaphoreType.DMA((cols + 1,)),
         ],
         compiler_params=pltpu.CompilerParams(
             collective_id=0, has_side_effects=True, vmem_limit_bytes=24 * 2**20

time: 19.3 us -> 20.3 us (1.052)
  Pallas kernels: 16.5 us -> 17.6 us
    pallas_call x1, Pallas kernels: 11.7 us -> 12.7 us  [per_device(): pl.pallas_call(functools.partial(messages_kernel, tiles, groups, cols, D)...]
where the time goes in v1:
time: 20.3 us; the launch traced here: 20.1 us
  Pallas kernels  17.6 us (87%)
  local copies, waits for them, and re-layouts  1.83 us (9%)
  between operations  0.65 us (3%)
    pallas_call x1, Pallas kernels, per_device(): pl.pallas_call(functools.partial(messages_kernel, tiles, groups, cols, D)...  12.7 us
    pallas_call x1, Pallas kernels, per_device(): pl.pallas_call(functools.partial(gates_kernel, cols, D), out_shape=(jax.S...  4.83 us
    unnamed x4, local copies, waits for them, and re-layouts  1.83 us

profile of v1, /device:TPU:1, one launch (start us, length us, event | category | flops | bytes accessed | tf_op | source)
XLA Modules:
  0.0 20.1 jit_solution(6795242220640131809)
XLA Ops:
  0.6 0.0 copy-start
  0.6 1.1 %copy-done = bf16[1,3,2,65536]{3,2,1,0:T(2,128)(2,1)S(1)} copy-done((bf16[1,3,2,65536]{3,2,1,0:T(2,128)(2,1)S(1)}, bf16[1,3,2,65536]{3,2,1,0:T(2,128)(2,1)}, u32[]{:S(2)}) %copy-start) | copy-done | bytes 786456
  1.8 0.0 copy-start.1
  1.8 0.7 %copy-done.1 = f32[1,3,4,256]{3,2,1,0:T(4,128)S(1)} copy-done((f32[1,3,4,256]{3,2,1,0:T(4,128)S(1)}, f32[1,3,4,256]{3,2,1,0:T(4,128)}, u32[]{:S(2)}) %copy-start.1) | copy-done | bytes 12312
  2.5 12.7 %shard_map.41 = (bf16[3,2,256,256]{3,2,1,0:T(8,128)(2,1)S(1)}, f32[3,16,192]{2,1,0:T(8,128)S(1)}, f32[192,16]{1,0:T(8,128)S(1)}) custom-call(bf16[3,1024,128]{2,1,0:T(8,128)(2,1)S(1)} %bitcast.12, f32[3,4,256]{2,1,0:T(4,128)S(1)} %bitcast.13), custom_call_target="tpu_custom_call" | custom-call | tf_op jit(solution)/shard_map/pallas_call | solution.py:502
  15.2 4.8 %shard_map.42 = (bf16[3,1024,128]{2,1,0:T(8,128)(2,1)}, f32[3,4,256]{2,1,0:T(4,128)}) custom-call(bf16[3,2,256,256]{3,2,1,0:T(8,128)(2,1)S(1)} %get-tuple-element.7.ax_ref, f32[3,16,192]{2,1,0:T(8,128)S(1)} %get-tuple-element.8.env_ref, f32[192,16]{1,0:T(8,128)S(1)} %get-tuple-element.9.in_ref), custom_call_target="tpu_custom_call" | custom-call | tf_op jit(solution)/shard_map/pallas_call | solution.py:532
Async XLA Ops:
  0.6 1.1 %copy-start = (bf16[1,3,2,65536]{3,2,1,0:T(2,128)(2,1)S(1)}, bf16[1,3,2,65536]{3,2,1,0:T(2,128)(2,1)}, u32[]{:S(2)}) copy-start(bf16[1,3,2,65536]{3,2,1,0:T(2,128)(2,1)} %param.2) | copy-start | bytes 2359300
  1.8 0.7 %copy-start.1 = (f32[1,3,4,256]{3,2,1,0:T(4,128)S(1)}, f32[1,3,4,256]{3,2,1,0:T(4,128)}, u32[]{:S(2)}) copy-start(f32[1,3,4,256]{3,2,1,0:T(4,128)} %param.3) | copy-start | bytes 36868

commit v2 on v1

--- a/solution.py
+++ b/solution.py
@@ -528,7 +528,10 @@
         compiler_params=pltpu.CompilerParams(
             collective_id=0, has_side_effects=True, vmem_limit_bytes=24 * 2**20
         ),
-    )(a, msg_in[0])
+    )(
+        pltpu.with_memory_space_constraint(a, pltpu.HBM),
+        pltpu.with_memory_space_constraint(msg_in[0], pltpu.HBM),
+    )
     out, messages = pl.pallas_call(
         functools.partial(gates_kernel, cols, D),
         out_shape=(

time: 20.3 us -> 19 us (0.936)
  local copies, waits for them, and re-layouts: 1.83 us -> 0 us
  Pallas kernels: 17.6 us -> 18.2 us
    unnamed x4 -> x0, local copies, waits for them, and re-layouts: 1.83 us -> none
    pallas_call x1, Pallas kernels: 12.7 us -> 13.4 us  [per_device(): pl.pallas_call(functools.partial(messages_kernel, tiles, groups, cols, D)...]
where the time goes in v2:
time: 19 us; the launch traced here: 18.8 us
  Pallas kernels  18.2 us (96%)
  between operations  0.64 us (3%)
    pallas_call x1, Pallas kernels, per_device(): pl.pallas_call(functools.partial(messages_kernel, tiles, groups, cols, D)...  13.4 us
    pallas_call x1, Pallas kernels, per_device(): pl.pallas_call(functools.partial(gates_kernel, cols, D), out_shape=(jax.S...  4.83 us

profile of v2, /device:TPU:1, one launch (start us, length us, event | category | flops | bytes accessed | tf_op | source)
XLA Modules:
  0.0 18.8 jit_solution(13688421263697280073)
XLA Ops:
  0.6 13.4 %shard_map.41 = (bf16[3,2,256,256]{3,2,1,0:T(8,128)(2,1)S(1)}, f32[3,16,192]{2,1,0:T(8,128)S(1)}, f32[192,16]{1,0:T(8,128)S(1)}) custom-call(bf16[3,1024,128]{2,1,0:T(8,128)(2,1)} %bitcast.12, f32[3,4,256]{2,1,0:T(4,128)} %bitcast.13), custom_call_target="tpu_custom_call" | custom-call | tf_op jit(solution)/shard_map/pallas_call | solution.py:502
  14.0 4.8 %shard_map.42 = (bf16[3,1024,128]{2,1,0:T(8,128)(2,1)}, f32[3,4,256]{2,1,0:T(4,128)}) custom-call(bf16[3,2,256,256]{3,2,1,0:T(8,128)(2,1)S(1)} %get-tuple-element.7.ax_ref, f32[3,16,192]{2,1,0:T(8,128)S(1)} %get-tuple-element.8.env_ref, f32[192,16]{1,0:T(8,128)S(1)} %get-tuple-element.9.in_ref), custom_call_target="tpu_custom_call" | custom-call | tf_op jit(solution)/shard_map/pallas_call | solution.py:535

commit v3 on v2

--- a/solution.py
+++ b/solution.py
@@ -68,7 +68,75 @@
     return one_hot(k == (p & (rows - 1)) * mixed + (p >> row_bits))
 
 
-def messages_kernel(tiles, groups, cols, D, a_hbm, msg_hbm, ax_ref, env_ref, mout_ref,
+def pick(value, index):
+    return jnp.take_along_axis(value, index, axis=1, mode="promise_in_bounds")
+
+
+def row_of(value, k):
+    return jnp.broadcast_to(value[k : k + 1, :], value.shape)
+
+
+def bond_weights(msg_sum, twist_sum):
+    D = msg_sum.shape[0]
+    lane = iota((D, LANES), 1)
+    row = iota((D, LANES), 0)
+    inner = lane & (D - 1)
+    start = lane - inner
+    turned = start + row
+    unit = jnp.where(inner == row, 1.0, 0.0).astype(F32)
+    g0, g1 = math.cosh(COUPLING), math.sinh(COUPLING)
+    cross = math.sqrt(g0 * g1)
+    root2 = math.sqrt(2.0)
+    halves = [
+        ((g0 * msg_sum + cross * twist_sum) / root2).astype(BF16).astype(F32),
+        ((cross * twist_sum + g1 * msg_sum) / root2).astype(BF16).astype(F32),
+    ]
+    squares = halves[0] * halves[0] + halves[1] * halves[1]
+    squares = jnp.broadcast_to(jnp.sum(squares, axis=0, keepdims=True), (D, LANES))
+    trace = jnp.sum(pick(squares, turned), axis=0, keepdims=True) + EPSILON
+
+    gram = None
+    rotated = []
+    for half in halves:
+        transposed = None
+        for k in range(D):
+            own = row_of(half, k)
+            column = pick(own, turned)
+            term = column * own
+            gram = term if gram is None else gram + term
+            placed = jnp.where(inner == k, column, 0.0)
+            transposed = placed if transposed is None else transposed + placed
+        rotated.append(transposed)
+
+    def columns(value):
+        return [pick(row_of(value, k), turned) for k in range(D)]
+
+    def times(left, right):
+        sums = [None] * 4
+        for k in range(D):
+            term = left[k] * row_of(right, k)
+            sums[k % 4] = term if sums[k % 4] is None else sums[k % 4] + term
+        return (sums[0] + sums[1]) + (sums[2] + sums[3])
+
+    state = gram / trace
+    for step in range(NS_STEPS - 2):
+        left = columns(state)
+        square = times(left, state)
+        rotated = [1.5 * v - 0.5 * times(left, v) for v in rotated]
+        state = times(left, 2.25 * unit - 1.5 * state + 0.25 * square)
+    left = columns(state)
+    rotated = [1.5 * v - 0.5 * times(left, v) for v in rotated]
+    again = rotated
+    for _ in range(2):
+        again = [1.5 * v - 0.5 * times(left, v) for v in again]
+    rotated = [1.5 * v - 0.5 * times(left, w) for v, w in zip(rotated, again)]
+    scale = 1.0 / jnp.sqrt(trace)
+    first = math.sqrt(g0) * rotated[0] * scale
+    second = math.sqrt(g1) * rotated[1] * scale
+    return [first + second, first - second]
+
+
+def messages_kernel(tiles, groups, cols, D, a_hbm, msg_hbm, ax_ref, env_ref, inner_ref, mout_ref,
            a_ref, msg_ref, x_ref, xt_ref, kron_ref, gram_ref,
            send_up, send_down, send_side, recv_up, recv_down, recv_side,
            send_sem, recv_sem, load_sem):
@@ -321,6 +389,10 @@
             routed.append(blocks)
         return routed
 
+    def lined(blocks):
+        spare = LANES // D - len(blocks)
+        return jnp.concatenate(blocks + [jnp.zeros((D, D), F32)] * spare, axis=1)
+
     incoming = edge
     for turn in range(ITERS):
         last = turn == ITERS - 1
@@ -344,114 +416,94 @@
                 ch, sh = math.cosh(FIELD), math.sinh(FIELD)
                 ax_ref[i, 0] = (ch * a0 + sh * a1).astype(BF16)
                 ax_ref[i, 1] = (ch * a1 + sh * a0).astype(BF16)
+        if last:
+            sums = [
+                lined([v[i * 4 + 3] + v[i * 4 + 5] for i in range(cols - 1)]) for v in values
+            ]
+            for s, weight in enumerate(bond_weights(*sums)):
+                inner_ref[s] = weight.astype(BF16).astype(F32)
         routed = finish(turn, copies, values)
         incoming = routed[0]
 
-    mout_ref[...] = jnp.concatenate(incoming, axis=0)
-    env_ref[0] = jnp.concatenate([o + n for o, n in zip(values[0], routed[0])], axis=1)
-    env_ref[1] = jnp.concatenate([o + n for o, n in zip(values[1], routed[1])], axis=1)
-    lane_w = iota((D, wide), 1)
-    leg_of = (lane_w >> shift) & 3
-    col_of = (lane_w >> (shift + 2)) + group * cols
-    at_edge = (
-        ((leg_of == 0) & (tile == 0))
-        | ((leg_of == 2) & (tile == tiles - 1))
-        | ((leg_of == 1) & (col_of == 0))
-        | ((leg_of == 3) & (col_of == groups * cols - 1))
-    )
-    env_ref[2] = jnp.where(at_edge, 1.0, 0.0).astype(F32)
-
-
-def gates_kernel(cols, D, ax_ref, env_ref, in_ref, out_hbm, mout_hbm,
+    outer = [i * 4 for i in range(cols)] + [i * 4 + 2 for i in range(cols)]
+    outer += [1, 4 * cols - 1]
+    for kind in range(2):
+        env_ref[kind] = lined([values[kind][m] + routed[kind][m] for m in outer])
+    for t in range(mout_ref.shape[0]):
+        mout_ref[t] = lined(incoming[t * 8 : t * 8 + 8])
+
+
+def gates_kernel(tiles, groups, cols, D, ax_ref, env_ref, inner_ref, in_ref, out_hbm, mout_hbm,
                  kron_ref, out_ref, mout_ref, store_sem):
+    tile = lax.axis_index("tile")
+    group = lax.axis_index("group")
     DD = D * D
     shift = D.bit_length() - 1
-    mixed = 2 * (DD // LANES)
+    halves = DD // LANES
+    mixed = 2 * halves
     rows = DD // mixed
-    legs = 4 * cols
-    wide = legs * D
-    lane = iota((D, DD), 1)
-    row = iota((D, DD), 0)
-    major = one_hot((lane >> shift) == row)
-    minor = one_hot((lane & (D - 1)) == row)
-    both = jnp.concatenate([major, minor], axis=1)
-
-    spread = select_dot(in_ref[...], minor, 3)
-    unfold_mask = (lane >> shift) == row
-    flat_rows = [
-        jnp.sum(
-            jnp.where(unfold_mask, spread[m * D : (m + 1) * D], 0.0), axis=0, keepdims=True
+    lane = iota((D, LANES), 1)
+    row = iota((D, LANES), 0)
+    inner = lane & (D - 1)
+    start = lane - inner
+    slot = lane >> shift
+
+    unit = jnp.where(inner == row, 1.0, 0.0).astype(F32)
+    at_edge = (
+        ((slot < cols) & (tile == 0))
+        | ((slot >= cols) & (slot < 2 * cols) & (tile == tiles - 1))
+        | ((slot == 2 * cols) & (group == 0))
+        | ((slot == 2 * cols + 1) & (group == groups - 1))
+    )
+    late = [
+        jnp.where(at_edge, unit, w).astype(BF16).astype(F32)
+        for w in bond_weights(env_ref[0], env_ref[1])
+    ]
+    early = [inner_ref[s] for s in range(2)]
+
+    unfold_mask = slot == (row & (LANES // D - 1))
+    flat_rows = []
+    for m in range(4 * cols):
+        value = in_ref[m // 8]
+        tiled = jnp.where(unfold_mask, pick(value, inner + (m % 8) * D), 0.0)
+        step = D // halves
+        flat_rows.append(
+            jnp.concatenate(
+                [
+                    jnp.sum(tiled[h * step : (h + 1) * step], axis=0, keepdims=True)
+                    for h in range(halves)
+                ],
+                axis=1,
+            )
         )
-        for m in range(legs)
-    ]
     mout_ref[...] = jnp.concatenate(flat_rows, axis=0).reshape(cols, 4, DD)
     store_msg = pltpu.make_async_copy(mout_ref, mout_hbm, store_sem.at[cols])
     store_msg.start()
 
-    g0, g1 = math.cosh(COUPLING), math.sinh(COUPLING)
-    cross = math.sqrt(g0 * g1)
-    root2 = math.sqrt(2.0)
-    msg_sum, twist_sum = env_ref[0], env_ref[1]
-    y_top = ((g0 * msg_sum + cross * twist_sum) / root2).astype(BF16)
-    y_bot = ((cross * twist_sum + g1 * msg_sum) / root2).astype(BF16)
-    y_both = jnp.concatenate([y_top, y_bot], axis=0)
-    same = (iota((wide, wide), 0) >> shift) == (iota((wide, wide), 1) >> shift)
-    same_bf = one_hot(same)
-    lane_w = iota((D, wide), 1)
-    unit = jnp.where((lane_w & (D - 1)) == iota((D, wide), 0), 1.0, 0.0).astype(F32)
-
-    def diagonal(value):
-        return jnp.concatenate([value] * legs, axis=0) * same_bf
-
-    def times(left, right):
-        count = left.shape[0]
-        (l_hi, l_lo), (r_hi, r_lo) = parts(left, 2), parts(right, 2)
-        main = dot(jnp.concatenate([l_hi, l_lo], axis=0), diagonal(r_hi))
-        return main[:count] + (main[count:] + dot(l_hi, diagonal(r_lo)))
-
-    full = jnp.where(same, dot_tn(y_both, y_both), 0.0)
-    gram = full[:D]
-    for m in range(1, legs):
-        gram = gram + full[m * D : (m + 1) * D]
-    diag = jnp.sum(gram * unit, axis=0, keepdims=True)
-    trace = select_dot(jnp.broadcast_to(diag, (8, wide)), same_bf, 3)[0:1] + EPSILON
-    current = gram / trace
-    factor = 1.5 * unit - 0.5 * current
-    inverse = factor
-    current = times(current, factor)
-    for step in range(1, NS_STEPS):
-        factor = 1.5 * unit - 0.5 * times(inverse, current)
-        if step < NS_STEPS - 1:
-            stepped = times(jnp.concatenate([inverse, current], axis=0), factor)
-            inverse, current = stepped[:D], stepped[D:]
-        else:
-            inverse = times(inverse, factor)
-    q_both = dot(y_both, diagonal(inverse.astype(BF16))) / jnp.sqrt(trace)
-    first = math.sqrt(g0) * q_both[:D]
-    second = math.sqrt(g1) * q_both[D:]
-    at_edge = env_ref[2] > 0.5
+    def by_major(value, m):
+        return jnp.concatenate(
+            [pick(value, m * D + slot + h * (LANES // D)) for h in range(halves)], axis=1
+        )
+
+    def by_minor(value, m):
+        part = pick(value, m * D + inner)
+        return jnp.concatenate([part] * halves, axis=1)
+
     scatter = permutation(DD, rows, mixed, 1)
-    spreads = []
-    for weight in (first + second, first - second):
-        weight = jnp.where(at_edge, unit, weight)
-        spreads.append(dot(weight.T.astype(BF16), both))
     stores = [
         pltpu.make_async_copy(out_ref.at[i], out_hbm.at[i], store_sem.at[i]) for i in range(cols)
     ]
+
     def gate(i):
-        m = i * 4
         gated = []
         for s in range(2):
-            w = spreads[s]
-            slot = (i * 2 + s) * 2
-            build_kron(
-                kron_ref, slot, w[(m + 2) * D : (m + 3) * D, :DD], w[(m + 3) * D : (m + 4) * D, DD:]
-            )
-            build_kron(
-                kron_ref, slot + 1, w[m * D : (m + 1) * D, :DD], w[(m + 1) * D : (m + 2) * D, DD:]
-            )
-            half = dot_nt(ax_ref[i, s], kron_ref[slot]).astype(BF16)
-            gated.append(dot(kron_ref[slot + 1], half).astype(BF16))
+            left = by_minor(late[s], 2 * cols) if i == 0 else by_minor(early[s], i - 1)
+            right = by_minor(late[s], 2 * cols + 1) if i == cols - 1 else by_minor(early[s], i)
+            at = (i * 2 + s) * 2
+            build_kron(kron_ref, at, by_major(late[s], cols + i), right)
+            build_kron(kron_ref, at + 1, by_major(late[s], i), left)
+            half = dot_nt(ax_ref[i, s], kron_ref[at]).astype(BF16)
+            gated.append(dot(kron_ref[at + 1], half).astype(BF16))
         return gated
 
     def emit(i, gated):
@@ -499,15 +551,16 @@
     legs = 4 * cols
     vmem = pl.BlockSpec(memory_space=pltpu.VMEM)
     hbm = pl.BlockSpec(memory_space=pltpu.HBM)
-    gated, env, stacked = pl.pallas_call(
+    gated, env, inner, stacked = pl.pallas_call(
         functools.partial(messages_kernel, tiles, groups, cols, D),
         out_shape=(
             jax.ShapeDtypeStruct((cols, 2, DD, DD), BF16),
-            jax.ShapeDtypeStruct((3, D, legs * D), F32),
-            jax.ShapeDtypeStruct((legs * D, D), F32),
+            jax.ShapeDtypeStruct((2, D, LANES), F32),
+            jax.ShapeDtypeStruct((2, D, LANES), F32),
+            jax.ShapeDtypeStruct((pl.cdiv(legs, LANES // D), D, LANES), F32),
         ),
         in_specs=[hbm, hbm],
-        out_specs=(vmem, vmem, vmem),
+        out_specs=(vmem, vmem, vmem, vmem),
         scratch_shapes=[
             pltpu.VMEM(a.shape, BF16),
             pltpu.VMEM((cols, 4, DD), F32),
@@ -533,12 +586,12 @@
         pltpu.with_memory_space_constraint(msg_in[0], pltpu.HBM),
     )
     out, messages = pl.pallas_call(
-        functools.partial(gates_kernel, cols, D),
+        functools.partial(gates_kernel, tiles, groups, cols, D),
         out_shape=(
             jax.ShapeDtypeStruct(a.shape, BF16),
             jax.ShapeDtypeStruct((cols, 4, DD), F32),
         ),
-        in_specs=[vmem, vmem, vmem],
+        in_specs=[vmem, vmem, vmem, vmem],
         out_specs=(hbm, hbm),
         scratch_shapes=[
             pltpu.VMEM((4 * cols, DD, DD), BF16),
@@ -547,7 +600,7 @@
             pltpu.SemaphoreType.DMA((cols + 1,)),
         ],
         compiler_params=pltpu.CompilerParams(vmem_limit_bytes=24 * 2**20),
-    )(gated, env, stacked)
+    )(gated, env, inner, stacked)
     out = out.reshape(cols, chunks, 2, LANES).transpose(0, 2, 1, 3)
     return out.reshape(1, cols, 2, size), messages[None]
 

time: 19 us -> 17.3 us (0.911)
  Pallas kernels: 18.2 us -> 16.5 us
    pallas_call x1, Pallas kernels: 4.83 us -> 3.09 us  [per_device(): pl.pallas_call(functools.partial(gates_kernel, tiles, groups, cols, D), o...]
where the time goes in v3:
time: 17.3 us; the launch traced here: 17.1 us
  Pallas kernels  16.5 us (95%)
  between operations  0.64 us (4%)
    pallas_call x1, Pallas kernels, per_device(): pl.pallas_call(functools.partial(messages_kernel, tiles, groups, cols, D)...  13.4 us
    pallas_call x1, Pallas kernels, per_device(): pl.pallas_call(functools.partial(gates_kernel, tiles, groups, cols, D), o...  3.09 us

profile of v3, /device:TPU:1, one launch (start us, length us, event | category | flops | bytes accessed | tf_op | source)
XLA Modules:
  0.0 17.1 jit_solution(6808003569511453789)
XLA Ops:
  0.6 13.4 %shard_map.41 = (bf16[3,2,256,256]{3,2,1,0:T(8,128)(2,1)S(1)}, f32[2,16,128]{2,1,0:T(8,128)S(1)}, f32[2,16,128]{2,1,0:T(8,128)S(1)}, f32[2,16,128]{2,1,0:T(8,128)S(1)}) custom-call(bf16[3,1024,128]{2,1,0:T(8,128)(2,1)} %bitcast.12, f32[3,4,256]{2,1,0:T(4,128)} %bitcast.13), custom_call_target="tpu_custom_call" | custom-call | tf_op jit(solution)/shard_map/pallas_call | solution.py:554
  14.0 3.1 %shard_map.42 = (bf16[3,1024,128]{2,1,0:T(8,128)(2,1)}, f32[3,4,256]{2,1,0:T(4,128)}) custom-call(bf16[3,2,256,256]{3,2,1,0:T(8,128)(2,1)S(1)} %get-tuple-element.8.ax_ref, f32[2,16,128]{2,1,0:T(8,128)S(1)} %get-tuple-element.9.env_ref, f32[2,16,128]{2,1,0:T(8,128)S(1)} %get-tuple-element.10.inner_ref, f32[2,16,128]{2,1,0:T(8,128)S(1)} %get-tuple-element.11.in_ref), custom_call_target="tpu_custom_call" | custom-call | tf_op jit(solution)/shard_map/pallas_call | solution.py:588

commit v4 on v3

v4 whole, which is shorter than its diff:
```python
import functools
import math

import jax
import jax.numpy as jnp
from jax import lax
from jax.experimental import pallas as pl
from jax.experimental.pallas import tpu as pltpu
from jax.sharding import PartitionSpec as P

ITERS = 2
NS_STEPS = 6
LANES = 128
EPSILON = 1e-06
COUPLING = 0.5
FIELD = 0.3
F32 = jnp.float32
BF16 = jnp.bfloat16
MESH = pl.DeviceIdType.MESH


def iota(shape, axis):
    return lax.broadcasted_iota(jnp.int32, shape, axis)


def dot(a, b):
    return jnp.dot(a, b, preferred_element_type=F32)


def dot_nt(a, b):
    return lax.dot_general(a, b, (((1,), (1,)), ((), ())), preferred_element_type=F32)


def dot_tn(a, b):
    return lax.dot_general(a, b, (((0,), (0,)), ((), ())), preferred_element_type=F32)


def parts(value, count):
    out = []
    for _ in range(count):
        piece = value.astype(BF16)
        out.append(piece)
        value = value - piece.astype(F32)
    return out


def select_dot(value, selector, count):
    total = None
    for piece in parts(value, count):
        term = dot(piece, selector)
        total = term if total is None else total + term
    return total


def one_hot(mask):
    return jnp.where(mask, 1.0, 0.0).astype(BF16)


def build_kron(kron_ref, slot, first, second):
    D = first.shape[0]
    for d in range(D):
        kron_ref[slot, d * D : (d + 1) * D, :] = (first[d : d + 1, :] * second).astype(BF16)


def pick(value, index):
    return jnp.take_along_axis(value, index, axis=1, mode="promise_in_bounds")


def row_of(value, k):
    return jnp.broadcast_to(value[k : k + 1, :], value.shape)


def bond_weights(msg_sum, twist_sum):
    D = msg_sum.shape[0]
    lane = iota((D, LANES), 1)
    row = iota((D, LANES), 0)
    inner = lane & (D - 1)
    start = lane - inner
    turned = start + row
    unit = jnp.where(inner == row, 1.0, 0.0).astype(F32)
    g0, g1 = math.cosh(COUPLING), math.sinh(COUPLING)
    cross = math.sqrt(g0 * g1)
    root2 = math.sqrt(2.0)
    halves = [
        ((g0 * msg_sum + cross * twist_sum) / root2).astype(BF16).astype(F32),
        ((cross * twist_sum + g1 * msg_sum) / root2).astype(BF16).astype(F32),
    ]
    squares = halves[0] * halves[0] + halves[1] * halves[1]
    squares = jnp.broadcast_to(jnp.sum(squares, axis=0, keepdims=True), (D, LANES))
    trace = jnp.sum(pick(squares, turned), axis=0, keepdims=True) + EPSILON

    gram = None
    rotated = []
    for half in halves:
        transposed = None
        for k in range(D):
            own = row_of(half, k)
            column = pick(own, turned)
            term = column * own
            gram = term if gram is None else gram + term
            placed = jnp.where(inner == k, column, 0.0)
            transposed = placed if transposed is None else transposed + placed
        rotated.append(transposed)

    def columns(value):
        return [pick(row_of(value, k), turned) for k in range(D)]

    def times(left, right):
        sums = [None] * 4
        for k in range(D):
            term = left[k] * row_of(right, k)
            sums[k % 4] = term if sums[k % 4] is None else sums[k % 4] + term
        return (sums[0] + sums[1]) + (sums[2] + sums[3])

    state = gram / trace
    for step in range(NS_STEPS - 2):
        left = columns(state)
        square = times(left, state)
        rotated = [1.5 * v - 0.5 * times(left, v) for v in rotated]
        state = times(left, 2.25 * unit - 1.5 * state + 0.25 * square)
    left = columns(state)
    rotated = [1.5 * v - 0.5 * times(left, v) for v in rotated]
    again = rotated
    for _ in range(2):
        again = [1.5 * v - 0.5 * times(left, v) for v in again]
    rotated = [1.5 * v - 0.5 * times(left, w) for v, w in zip(rotated, again)]
    scale = 1.0 / jnp.sqrt(trace)
    first = math.sqrt(g0) * rotated[0] * scale
    second = math.sqrt(g1) * rotated[1] * scale
    return [first + second, first - second]


def unmixing(D, mixed, out_axis):
    DD = D * D
    sub = D // mixed
    p, k = iota((DD, DD), out_axis), iota((DD, DD), 1 - out_axis)
    low = p & (D - 1)
    mid = (p >> (D.bit_length() - 1)) & (sub - 1)
    top = p >> (D * sub).bit_length() - 1
    return one_hot(k == low * D + mid * mixed + top)


def messages_kernel(tiles, groups, cols, D, a_hbm, msg_hbm, ax_ref, env_ref, inner_ref, mout_ref,
           a_ref, msg_ref, x_ref, xt_ref, x2_ref, x2t_ref, kron_ref, gram_ref,
           send_v0, send_v1, send_s0, send_s1, up_0, up_1, down_0, down_1, side_0, side_1,
           send_sem, recv_sem, load_sem):
    loads = [pltpu.make_async_copy(msg_hbm, msg_ref, load_sem.at[cols])]
    loads += [
        pltpu.make_async_copy(a_hbm.at[i], a_ref.at[i], load_sem.at[i]) for i in range(cols)
    ]
    for load in loads:
        load.start()
    tile = lax.axis_index("tile")
    group = lax.axis_index("group")
    DD = D * D
    shift = D.bit_length() - 1
    halves = DD // LANES
    mixed = 2 * halves
    sub = D // mixed
    per = LANES // D
    legs = 4 * cols
    crossing = jnp.where(group == 0, cols - 1, 0)
    closed = jnp.where(group == 0, 0, cols - 1)
    order = list(range(1, cols - 1)) + [closed, crossing]
    has_up = tile > 0
    has_down = tile < tiles - 1

    barrier = pltpu.get_barrier_semaphore()

    @pl.when(has_up)
    def _():
        pl.semaphore_signal(barrier, inc=1, device_id={"tile": tile - 1}, device_id_type=MESH)

    @pl.when(has_down)
    def _():
        pl.semaphore_signal(barrier, inc=1, device_id={"tile": tile + 1}, device_id_type=MESH)

    pl.semaphore_signal(barrier, inc=1, device_id={"group": 1 - group}, device_id_type=MESH)

    lane = iota((D, LANES), 1)
    row = iota((D, LANES), 0)
    within = lane & (D - 1)
    turned = lane - within + row
    slot = lane >> shift
    gather = unmixing(D, mixed, 0)
    fold_minor = one_hot((iota((LANES, LANES), 0) & (D - 1)) == (iota((LANES, LANES), 1) & (D - 1)))
    fold_major = one_hot((iota((DD, LANES), 0) >> shift) == (iota((DD, LANES), 1) & (D - 1)))

    def placed(entries):
        total = jnp.zeros((D, LANES), F32)
        for where, value in entries:
            total = jnp.where(slot == where, value, total)
        return total

    def by_major(value, m):
        return jnp.concatenate([pick(value, m * D + slot + h * per) for h in range(halves)], axis=1)

    def by_minor(value, m):
        return jnp.concatenate([pick(value, m * D + within)] * halves, axis=1)

    def rounded(value):
        return value.astype(BF16).astype(F32)

    def reduce_major(gram, weight):
        total = gram[:D] * weight[0:1, :]
        for d in range(1, D):
            total = total + gram[d * D : (d + 1) * D] * weight[d : d + 1, :]
        return total

    def reduce_minor(gram, weight):
        return jnp.concatenate(
            [
                jnp.sum(gram[d * D : (d + 1) * D] * weight, axis=0, keepdims=True)
                for d in range(D)
            ],
            axis=0,
        )

    def kinds_of(totals):
        if len(totals) == 1:
            return totals
        return [totals[0] + totals[1], totals[0] - totals[1]]

    def folded(totals, selector):
        pieces = []
        for total in totals:
            if selector is fold_minor:
                joined = total[:, :LANES]
                for h in range(1, halves):
                    joined = joined + total[:, h * LANES : (h + 1) * LANES]
                total = joined
            pieces += parts(total, 2)
        out = dot(jnp.concatenate(pieces, axis=0), selector)
        return [
            out[2 * n * D : (2 * n + 1) * D] + out[(2 * n + 1) * D : (2 * n + 2) * D]
            for n in range(len(totals))
        ]

    def minors(totals):
        count = len(totals[0])
        flat = folded([v for t in totals for v in t], fold_minor)
        return [flat[n * count : (n + 1) * count] for n in range(len(totals))]

    def majors(totals):
        count = len(totals[0])
        flat = folded([v for t in totals for v in t], fold_major)
        return [flat[n * count : (n + 1) * count] for n in range(len(totals))]

    def normalised(values):
        power = jnp.sum(values[0] * values[0], axis=0, keepdims=True)
        power = pick(jnp.broadcast_to(power, (D, LANES)), turned)
        power = jnp.sum(power, axis=0, keepdims=True) / DD
        scale = 1.0 / jnp.sqrt(power + EPSILON)
        return [v * scale for v in values]

    def upright(ups, downs, kind):
        return placed(
            [(i, ups[i][kind]) for i in range(cols)]
            + [(cols + i, downs[i][kind]) for i in range(cols)]
        )

    def copy(src, dst, turn, k, device):
        return pltpu.make_async_remote_copy(
            src_ref=src, dst_ref=dst, send_sem=send_sem.at[turn, k],
            recv_sem=recv_sem.at[turn, k], device_id=device, device_id_type=MESH,
        )

    def rows_copies(turn, src, up_dst, down_dst):
        to_up = copy(src, down_dst, turn, 0, {"tile": tile - 1})
        to_down = copy(src, up_dst, turn, 1, {"tile": tile + 1})

        @pl.when(has_up)
        def _():
            to_up.start()

        @pl.when(has_down)
        def _():
            to_down.start()

        return to_up, to_down

    def rows_arrive(copies, up_dst, down_dst, edges):
        to_up, to_down = copies

        @pl.when(has_up)
        def _():
            to_up.wait_send()
            to_down.wait_recv()

        @pl.when(jnp.logical_not(has_up))
        def _():
            up_dst[...] = edges

        @pl.when(has_down)
        def _():
            to_down.wait_send()
            to_up.wait_recv()

        @pl.when(jnp.logical_not(has_down))
        def _():
            down_dst[...] = edges

        above, below = up_dst[...], down_dst[...]
        return [
            jnp.where(slot < cols, above[k * D : (k + 1) * D], below[k * D : (k + 1) * D])
            for k in range(above.shape[0] // D)
        ]

    from_left = (slot == 0) | (slot == 2 * cols)
    from_right = (slot == 2 * cols - 1) | (slot == 2 * cols + 1)

    def sides_arrive(to_side, dst, local, edges):
        to_side.wait()
        got = dst[...]
        out = []
        for k, (value, edge) in enumerate(zip(local, edges)):
            other = got[k * D : (k + 1) * D]
            value = jnp.where(from_left, jnp.where(group == 0, edge, other), value)
            out.append(
                jnp.where(from_right, jnp.where(group == groups - 1, edge, other), value)
            )
        return out

    loads[0].wait()
    spot = (row & (per - 1)) * D + within
    flat = msg_ref[...].reshape(legs, DD)

    def unfolded(m):
        source = jnp.concatenate(
            [
                jnp.broadcast_to(flat[m : m + 1, h * LANES : (h + 1) * LANES], (per, LANES))
                for h in range(halves)
            ],
            axis=0,
        )
        return pick(source, spot)

    singles = [unfolded(m) for m in range(legs)]
    edge_rows = placed(
        [(i, singles[4 * i]) for i in range(cols)]
        + [(cols + i, singles[4 * i + 2]) for i in range(cols)]
    )
    edge_sides = placed(
        [(i, singles[4 * i + 1]) for i in range(cols)]
        + [(cols + i, singles[4 * i + 3]) for i in range(cols)]
    )

    def unmix(i):
        for b in range(0, mixed, 2):
            pair = jnp.concatenate(
                [
                    jnp.concatenate(
                        [
                            a_ref[i, u * D * mixed + (b + c) * D : u * D * mixed + (b + c + 1) * D]
                            for u in range(D)
                        ],
                        axis=0,
                    )
                    for c in range(2)
                ],
                axis=1,
            )
            block = dot(gather, pair).astype(BF16)
            span = sub * D
            for c in range(2):
                for g in range(mixed):
                    x_ref[
                        i,
                        g % 2,
                        (b + c) * span : (b + c + 1) * span,
                        (g // 2) * LANES : (g // 2 + 1) * LANES,
                    ] = block[g * span : (g + 1) * span, c * LANES : (c + 1) * LANES]
        for s in range(2):
            xt_ref[i, s] = x_ref[i, s].T

    def relayout(i, s):
        for h in range(halves):
            for lh in range(halves):
                values = [
                    x_ref[
                        i, s, (lh * per + k) * D : (lh * per + k + 1) * D,
                        h * LANES : (h + 1) * LANES,
                    ]
                    for k in range(per)
                ]
                step = 1
                while step < per:
                    high = (slot & step) != 0
                    out = list(values)
                    for a in range(per):
                        if a & step:
                            continue
                        b = a | step
                        low_up = pltpu.roll(values[b], D * step, 1)
                        high_down = pltpu.roll(values[a], LANES - D * step, 1)
                        out[a] = jnp.where(high, low_up, values[a])
                        out[b] = jnp.where(high, values[b], high_down)
                    values = out
                    step *= 2
                for d in range(per):
                    x2_ref[
                        i, s, (h * per + d) * D : (h * per + d + 1) * D,
                        lh * LANES : (lh + 1) * LANES,
                    ] = values[d]
        x2t_ref[i, s] = x2_ref[i, s].T

    v_rows, v_sides = rounded(edge_rows), rounded(edge_sides)
    ups, downs = [], []
    weights = []
    for i in range(cols):
        loads[1 + i].wait()
        unmix(i)
        w_up, w_down = by_minor(v_rows, i), by_major(v_rows, cols + i)
        w_left, w_right = by_major(v_sides, i), by_minor(v_sides, cols + i)
        weights.append((w_up, w_down))
        build_kron(kron_ref, 2 * i, w_down, w_right)
        build_kron(kron_ref, 2 * i + 1, w_left, w_up)
        for path, (left, right) in enumerate(((x_ref, xt_ref), (xt_ref, x_ref))):
            y = [dot(left[i, s], kron_ref[2 * i + path]).astype(BF16) for s in range(2)]
            gram_ref[2 * i + path, 0] = dot(y[0], right[i, 0]) + dot(y[1], right[i, 1])
        ups.append([reduce_major(gram_ref[2 * i, 0], w_left)])
        downs.append([reduce_minor(gram_ref[2 * i + 1, 0], w_right)])
    ups, downs = minors(ups), majors(downs)
    send_v0[...] = normalised([upright(downs, ups, 0)])[0]

    inside = jnp.logical_and(has_up, has_down)

    @pl.when(inside)
    def _():
        pl.semaphore_wait(barrier, 3)

    @pl.when(jnp.logical_not(inside))
    def _():
        pl.semaphore_wait(barrier, 2)

    rows_0 = rows_copies(0, send_v0, up_0, down_0)

    lefts = majors([[reduce_minor(gram_ref[2 * i, 0], weights[i][0])] for i in range(cols)])
    rights = minors([[reduce_major(gram_ref[2 * i + 1, 0], weights[i][1])] for i in range(cols)])
    send_s0[...] = normalised([jnp.where(from_left, rights[cols - 1][0], lefts[0][0])])[0]
    sides_0 = copy(send_s0, side_0, 0, 2, {"group": 1 - group})
    sides_0.start()

    def inner_view(lefts, rights, kind):
        return placed(
            [(i, rights[i - 1][kind]) for i in range(1, cols)]
            + [(cols + i, lefts[i + 1][kind]) for i in range(cols - 1)]
        )

    n_sides = normalised([inner_view(lefts, rights, 0)])
    for i in range(cols):
        for s in range(2):
            relayout(i, s)
    for i in range(cols):
        a0, a1 = x_ref[i, 0].astype(F32), x_ref[i, 1].astype(F32)
        ch, sh = math.cosh(FIELD), math.sinh(FIELD)
        ax_ref[i, 0] = (ch * a0 + sh * a1).astype(BF16)
        ax_ref[i, 1] = (ch * a1 + sh * a0).astype(BF16)

    side_weights = []

    def paired(j, kron, left, right, at):
        i = order[j]
        for s in range(2):
            y = dot(left[i, s], kron_ref[kron]).astype(BF16)
            gram_ref[at, s] = dot(y, right[i, s])

    for j in range(cols):
        if j == cols - 1:
            n_sides = sides_arrive(sides_0, side_0, n_sides, [edge_sides])
        v_sides = rounded(n_sides[0]) if j == cols - 1 else rounded(jnp.where(
            from_left | from_right, edge_sides, n_sides[0]
        ))
        i = order[j]
        w_left, w_right = by_major(v_sides, i), by_minor(v_sides, cols + i)
        side_weights.append((w_left, w_right))
        build_kron(kron_ref, 2 * j, w_left, w_right)
        paired(j, 2 * j, x2_ref, x2t_ref, 2 * j)

    n_rows = rows_arrive(rows_0, up_0, down_0, edge_rows)
    v_rows = rounded(n_rows[0])
    ups, downs, weights = [], [], []
    for j in range(cols):
        i = order[j]
        w_up, w_down = by_minor(v_rows, i), by_major(v_rows, cols + i)
        weights.append((w_up, w_down))
        ups.append(kinds_of([reduce_major(gram_ref[2 * j, s], w_down) for s in range(2)]))
        downs.append(kinds_of([reduce_minor(gram_ref[2 * j, s], w_up) for s in range(2)]))
    ups, downs = minors(ups), majors(downs)

    def ordered(above, below, kind):
        return placed(
            [(order[j], above[j][kind]) for j in range(cols)]
            + [(cols + order[j], below[j][kind]) for j in range(cols)]
        )

    out_rows = normalised([ordered(downs, ups, k) for k in range(2)])
    for k in range(2):
        send_v1[k * D : (k + 1) * D] = out_rows[k]
    rows_1 = rows_copies(1, send_v1, up_1, down_1)
    o_rows = normalised([ordered(ups, downs, k) for k in range(2)])

    def horizontal(j):
        build_kron(kron_ref, 2 * j + 1, weights[j][1], weights[j][0])
        paired(j, 2 * j + 1, x2t_ref, x2_ref, 2 * j + 1)
        w_left, w_right = side_weights[j]
        left = kinds_of([reduce_minor(gram_ref[2 * j + 1, s], w_right) for s in range(2)])
        right = kinds_of([reduce_major(gram_ref[2 * j + 1, s], w_left) for s in range(2)])
        return left, right

    left, right = horizontal(cols - 1)
    (left,), (right,) = majors([left]), minors([right])
    out_sides = normalised([jnp.where(from_left, right[k], left[k]) for k in range(2)])
    for k in range(2):
        send_s1[k * D : (k + 1) * D] = out_sides[k]
    sides_1 = copy(send_s1, side_1, 1, 2, {"group": 1 - group})
    sides_1.start()
    others = [horizontal(j) for j in range(cols - 1)]
    lefts = majors([o[0] for o in others]) + [left]
    rights = minors([o[1] for o in others]) + [right]

    def own_sides(kind):
        base = placed(
            [(order[j], lefts[j][kind]) for j in range(cols)]
            + [(cols + order[j], rights[j][kind]) for j in range(cols)]
        )
        base = jnp.where((slot == 2 * cols) & (group == groups - 1), lefts[-1][kind], base)
        return jnp.where((slot == 2 * cols + 1) & (group == 0), rights[-1][kind], base)

    def other_sides(kind):
        entries = []
        for j, i in enumerate(order):
            entries.append((jnp.where(i == 0, -1, cols + i - 1), lefts[j][kind]))
            entries.append((jnp.where(i == cols - 1, -1, i + 1), rights[j][kind]))
        return placed(entries)

    o_sides = normalised([own_sides(k) for k in range(2)])
    n_sides = normalised([other_sides(k) for k in range(2)])
    for s, weight in enumerate(bond_weights(*[o + n for o, n in zip(o_sides, n_sides)])):
        inner_ref[s] = rounded(weight)
    zero = jnp.zeros((D, LANES), F32)
    n_sides = sides_arrive(sides_1, side_1, n_sides, [edge_sides, zero])
    n_rows = rows_arrive(rows_1, up_1, down_1, jnp.concatenate([edge_rows, zero], axis=0))
    for k in range(2):
        env_ref[k] = jnp.where(
            slot < 2 * cols, o_rows[k] + n_rows[k], o_sides[k] + n_sides[k]
        )
    mout_ref[0] = n_rows[0]
    mout_ref[1] = n_sides[0]


def gates_kernel(tiles, groups, cols, D, ax_ref, env_ref, inner_ref, in_ref, out_hbm, mout_hbm,
                 kron_ref, out_ref, mout_ref, store_sem):
    tile = lax.axis_index("tile")
    group = lax.axis_index("group")
    DD = D * D
    shift = D.bit_length() - 1
    halves = DD // LANES
    mixed = 2 * halves
    rows = DD // mixed
    lane = iota((D, LANES), 1)
    row = iota((D, LANES), 0)
    inner = lane & (D - 1)
    start = lane - inner
    slot = lane >> shift

    unit = jnp.where(inner == row, 1.0, 0.0).astype(F32)
    at_edge = (
        ((slot < cols) & (tile == 0))
        | ((slot >= cols) & (slot < 2 * cols) & (tile == tiles - 1))
        | ((slot == 2 * cols) & (group == 0))
        | ((slot == 2 * cols + 1) & (group == groups - 1))
    )
    late = [
        jnp.where(at_edge, unit, w).astype(BF16).astype(F32)
        for w in bond_weights(env_ref[0], env_ref[1])
    ]
    early = [inner_ref[s] for s in range(2)]

    unfold_mask = slot == (row & (LANES // D - 1))
    flat_rows = []
    for m in range(4 * cols):
        at = m // 4 + (cols if m % 4 >= 2 else 0)
        tiled = jnp.where(unfold_mask, pick(in_ref[m % 2], inner + at * D), 0.0)
        step = D // halves
        flat_rows.append(
            jnp.concatenate(
                [
                    jnp.sum(tiled[h * step : (h + 1) * step], axis=0, keepdims=True)
                    for h in range(halves)
                ],
                axis=1,
            )
        )
    mout_ref[...] = jnp.concatenate(flat_rows, axis=0).reshape(cols, 4, DD)
    store_msg = pltpu.make_async_copy(mout_ref, mout_hbm, store_sem.at[cols])
    store_msg.start()

    def by_major(value, m):
        return jnp.concatenate(
            [pick(value, m * D + slot + h * (LANES // D)) for h in range(halves)], axis=1
        )

    def by_minor(value, m):
        part = pick(value, m * D + inner)
        return jnp.concatenate([part] * halves, axis=1)

    scatter = unmixing(D, mixed, 1)
    stores = [
        pltpu.make_async_copy(out_ref.at[i], out_hbm.at[i], store_sem.at[i]) for i in range(cols)
    ]

    def gate(i):
        gated = []
        for s in range(2):
            left = by_major(late[s], 2 * cols) if i == 0 else by_major(early[s], i)
            right = (
                by_minor(late[s], 2 * cols + 1) if i == cols - 1 else by_minor(early[s], i + 1)
            )
            at = (i * 2 + s) * 2
            build_kron(kron_ref, at, by_major(late[s], cols + i), right)
            build_kron(kron_ref, at + 1, left, by_minor(late[s], i))
            half = dot_nt(ax_ref[i, s], kron_ref[at]).astype(BF16)
            gated.append(dot(kron_ref[at + 1], half).astype(BF16))
        return gated

    def emit(i, gated):
        for b in range(0, mixed, 2):
            block = jnp.concatenate(
                [
                    jnp.concatenate(
                        [
                            gated[g % 2][
                                (b + c) * rows : (b + c + 1) * rows,
                                (g // 2) * LANES : (g // 2 + 1) * LANES,
                            ]
                            for c in range(2)
                        ],
                        axis=1,
                    )
                    for g in range(mixed)
                ],
                axis=0,
            )
            done = dot(scatter, block).astype(BF16)
            for c in range(2):
                for u in range(D):
                    at = u * D * mixed + (b + c) * D
                    out_ref[i, at : at + D, :] = done[
                        u * D : (u + 1) * D, c * LANES : (c + 1) * LANES
                    ]
        stores[i].start()

    waiting = gate(0)
    for i in range(cols):
        following = gate(i + 1) if i + 1 < cols else None
        emit(i, waiting)
        waiting = following
    for store in stores + [store_msg]:
        store.wait()


def per_device(tiles, groups, site_tensors, msg_in):
    _, cols, _, size = site_tensors.shape
    DD = msg_in.shape[-1]
    D = math.isqrt(DD)
    chunks = size // LANES
    a = site_tensors.reshape(cols, 2, chunks, LANES).transpose(0, 2, 1, 3)
    a = a.reshape(cols, 2 * chunks, LANES)
    vmem = pl.BlockSpec(memory_space=pltpu.VMEM)
    hbm = pl.BlockSpec(memory_space=pltpu.HBM)
    gated, env, inner, stacked = pl.pallas_call(
        functools.partial(messages_kernel, tiles, groups, cols, D),
        out_shape=(
            jax.ShapeDtypeStruct((cols, 2, DD, DD), BF16),
            jax.ShapeDtypeStruct((2, D, LANES), F32),
            jax.ShapeDtypeStruct((2, D, LANES), F32),
            jax.ShapeDtypeStruct((2, D, LANES), F32),
        ),
        in_specs=[hbm, hbm],
        out_specs=(vmem, vmem, vmem, vmem),
        scratch_shapes=[
            pltpu.VMEM(a.shape, BF16),
            pltpu.VMEM((cols, 4, DD), F32),
            pltpu.VMEM((cols, 2, DD, DD), BF16),
            pltpu.VMEM((cols, 2, DD, DD), BF16),
            pltpu.VMEM((cols, 2, DD, DD), BF16),
            pltpu.VMEM((cols, 2, DD, DD), BF16),
            pltpu.VMEM((2 * cols, DD, DD), BF16),
            pltpu.VMEM((2 * cols, 2, DD, DD), F32),
        ]
        + [
            pltpu.VMEM(((1 + turn) * D, LANES), F32) for _ in range(5) for turn in range(ITERS)
        ]
        + [
            pltpu.SemaphoreType.DMA((ITERS, 3)),
            pltpu.SemaphoreType.DMA((ITERS, 3)),
            pltpu.SemaphoreType.DMA((cols + 1,)),
        ],
        compiler_params=pltpu.CompilerParams(
            collective_id=0, has_side_effects=True, vmem_limit_bytes=24 * 2**20
        ),
    )(
        pltpu.with_memory_space_constraint(a, pltpu.HBM),
        pltpu.with_memory_space_constraint(msg_in[0], pltpu.HBM),
    )
    out, messages = pl.pallas_call(
        functools.partial(gates_kernel, tiles, groups, cols, D),
        out_shape=(
            jax.ShapeDtypeStruct(a.shape, BF16),
            jax.ShapeDtypeStruct((cols, 4, DD), F32),
        ),
        in_specs=[vmem, vmem, vmem, vmem],
        out_specs=(hbm, hbm),
        scratch_shapes=[
            pltpu.VMEM((4 * cols, DD, DD), BF16),
            pltpu.VMEM(a.shape, BF16),
            pltpu.VMEM((cols, 4, DD), F32),
            pltpu.SemaphoreType.DMA((cols + 1,)),
        ],
        compiler_params=pltpu.CompilerParams(vmem_limit_bytes=24 * 2**20),
    )(gated, env, inner, stacked)
    out = out.reshape(cols, chunks, 2, LANES).transpose(0, 2, 1, 3)
    return out.reshape(1, cols, 2, size), messages[None]


def solution(mesh):
    spec = P("tile", "group", None, None)
    return jax.shard_map(
        functools.partial(per_device, mesh.shape["tile"], mesh.shape["group"]),
        mesh=mesh, in_specs=(spec, spec), out_specs=(spec, spec), check_vma=False,
    )
```

time: 17.3 us -> 16.6 us (0.960)
  the two profiles are of different devices: /device:TPU:1 before, /device:TPU:0 now
where the time goes in v4:
time: 16.6 us; the launch traced here: 16.4 us
  Pallas kernels  15.8 us (95%)
  between operations  0.64 us (4%)
    pallas_call x1, Pallas kernels, per_device(): pl.pallas_call(functools.partial(messages_kernel, tiles, groups, cols, D)...  12.7 us
    pallas_call x1, Pallas kernels, per_device(): pl.pallas_call(functools.partial(gates_kernel, tiles, groups, cols, D), o...  3.09 us

profile of v4, /device:TPU:0, one launch (start us, length us, event | category | flops | bytes accessed | tf_op | source)
XLA Modules:
  0.0 16.4 jit_solution(2311859246964286088)
XLA Ops:
  0.6 12.7 %shard_map.41 = (bf16[3,2,256,256]{3,2,1,0:T(8,128)(2,1)S(1)}, f32[2,16,128]{2,1,0:T(8,128)S(1)}, f32[2,16,128]{2,1,0:T(8,128)S(1)}, f32[2,16,128]{2,1,0:T(8,128)S(1)}) custom-call(bf16[3,1024,128]{2,1,0:T(8,128)(2,1)} %bitcast.12, f32[3,4,256]{2,1,0:T(4,128)} %bitcast.13), custom_call_target="tpu_custom_call" | custom-call | tf_op jit(solution)/shard_map/pallas_call | solution.py:672
  13.3 3.1 %shard_map.42 = (bf16[3,1024,128]{2,1,0:T(8,128)(2,1)}, f32[3,4,256]{2,1,0:T(4,128)}) custom-call(bf16[3,2,256,256]{3,2,1,0:T(8,128)(2,1)S(1)} %get-tuple-element.8.ax_ref, f32[2,16,128]{2,1,0:T(8,128)S(1)} %get-tuple-element.9.env_ref, f32[2,16,128]{2,1,0:T(8,128)S(1)} %get-tuple-element.10.inner_ref, f32[2,16,128]{2,1,0:T(8,128)S(1)} %get-tuple-element.11.in_ref), custom_call_target="tpu_custom_call" | custom-call | tf_op jit(solution)/shard_map/pallas_call | solution.py:707

commit v5 on v4

--- a/solution.py
+++ b/solution.py
@@ -207,14 +207,30 @@
             total = total + gram[d * D : (d + 1) * D] * weight[d : d + 1, :]
         return total
 
+    sublane = iota((8, DD), 0)
+
     def reduce_minor(gram, weight):
-        return jnp.concatenate(
-            [
-                jnp.sum(gram[d * D : (d + 1) * D] * weight, axis=0, keepdims=True)
-                for d in range(D)
-            ],
-            axis=0,
-        )
+        blocks = []
+        for d in range(D):
+            block = gram[d * D : (d + 1) * D] * weight
+            total = block[:8]
+            for h in range(1, D // 8):
+                total = total + block[h * 8 : (h + 1) * 8]
+            blocks.append(total)
+        out = []
+        for base in range(0, D, 8):
+            level = blocks[base : base + 8]
+            step = 1
+            while len(level) > 1:
+                low = (sublane & step) == 0
+                level = [
+                    jnp.where(low, level[n], level[n + 1])
+                    + pltpu.roll(jnp.where(low, level[n + 1], level[n]), step, 0)
+                    for n in range(0, len(level), 2)
+                ]
+                step *= 2
+            out.append(level[0])
+        return jnp.concatenate(out, axis=0)
 
     def kinds_of(totals):
         if len(totals) == 1:
@@ -370,8 +386,6 @@
                         (b + c) * span : (b + c + 1) * span,
                         (g // 2) * LANES : (g // 2 + 1) * LANES,
                     ] = block[g * span : (g + 1) * span, c * LANES : (c + 1) * LANES]
-        for s in range(2):
-            xt_ref[i, s] = x_ref[i, s].T
 
     def relayout(i, s):
         for h in range(halves):
@@ -405,23 +419,44 @@
         x2t_ref[i, s] = x2_ref[i, s].T
 
     v_rows, v_sides = rounded(edge_rows), rounded(edge_sides)
-    ups, downs = [], []
     weights = []
     for i in range(cols):
-        loads[1 + i].wait()
-        unmix(i)
         w_up, w_down = by_minor(v_rows, i), by_major(v_rows, cols + i)
         w_left, w_right = by_major(v_sides, i), by_minor(v_sides, cols + i)
-        weights.append((w_up, w_down))
+        weights.append((w_up, w_down, w_left, w_right))
         build_kron(kron_ref, 2 * i, w_down, w_right)
         build_kron(kron_ref, 2 * i + 1, w_left, w_up)
-        for path, (left, right) in enumerate(((x_ref, xt_ref), (xt_ref, x_ref))):
+    for load in loads[1:]:
+        load.wait()
+    for i in range(cols):
+        unmix(i)
+    for i in range(cols):
+        for s in range(2):
+            xt_ref[i, s] = x_ref[i, s].T
+    sides_of = ((x_ref, xt_ref), (xt_ref, x_ref))
+    for path, (left, right) in enumerate(sides_of):
+        for i in range(cols):
             y = [dot(left[i, s], kron_ref[2 * i + path]).astype(BF16) for s in range(2)]
-            gram_ref[2 * i + path, 0] = dot(y[0], right[i, 0]) + dot(y[1], right[i, 1])
-        ups.append([reduce_major(gram_ref[2 * i, 0], w_left)])
-        downs.append([reduce_minor(gram_ref[2 * i + 1, 0], w_right)])
-    ups, downs = minors(ups), majors(downs)
+            gram_ref[2 * i + path, 0] = dot(
+                jnp.concatenate(y, axis=1), right[i].reshape(2 * DD, DD)
+            )
+
+    def outer(i, leg):
+        w_up, w_down, w_left, w_right = weights[i]
+        if leg == 0:
+            return [reduce_major(gram_ref[2 * i, 0], w_left)]
+        if leg == 1:
+            return [reduce_minor(gram_ref[2 * i, 0], w_up)]
+        if leg == 2:
+            return [reduce_minor(gram_ref[2 * i + 1, 0], w_right)]
+        return [reduce_major(gram_ref[2 * i + 1, 0], w_down)]
+
+    first_minors = minors([outer(i, 0) for i in range(cols)] + [outer(cols - 1, 3)])
+    first_majors = majors([outer(i, 2) for i in range(cols)] + [outer(0, 1)])
+    ups, right_last = first_minors[:cols], first_minors[cols]
+    downs, left_first = first_majors[:cols], first_majors[cols]
     send_v0[...] = normalised([upright(downs, ups, 0)])[0]
+    send_s0[...] = normalised([jnp.where(from_left, right_last[0], left_first[0])])[0]
 
     inside = jnp.logical_and(has_up, has_down)
 
@@ -434,12 +469,15 @@
         pl.semaphore_wait(barrier, 2)
 
     rows_0 = rows_copies(0, send_v0, up_0, down_0)
-
-    lefts = majors([[reduce_minor(gram_ref[2 * i, 0], weights[i][0])] for i in range(cols)])
-    rights = minors([[reduce_major(gram_ref[2 * i + 1, 0], weights[i][1])] for i in range(cols)])
-    send_s0[...] = normalised([jnp.where(from_left, rights[cols - 1][0], lefts[0][0])])[0]
     sides_0 = copy(send_s0, side_0, 0, 2, {"group": 1 - group})
     sides_0.start()
+
+    for i in range(cols):
+        for s in range(2):
+            relayout(i, s)
+
+    lefts = [left_first] + majors([outer(i, 1) for i in range(1, cols)])
+    rights = minors([outer(i, 3) for i in range(cols - 1)]) + [right_last]
 
     def inner_view(lefts, rights, kind):
         return placed(
@@ -448,14 +486,6 @@
         )
 
     n_sides = normalised([inner_view(lefts, rights, 0)])
-    for i in range(cols):
-        for s in range(2):
-            relayout(i, s)
-    for i in range(cols):
-        a0, a1 = x_ref[i, 0].astype(F32), x_ref[i, 1].astype(F32)
-        ch, sh = math.cosh(FIELD), math.sinh(FIELD)
-        ax_ref[i, 0] = (ch * a0 + sh * a1).astype(BF16)
-        ax_ref[i, 1] = (ch * a1 + sh * a0).astype(BF16)
 
     side_weights = []
 
@@ -476,6 +506,13 @@
         side_weights.append((w_left, w_right))
         build_kron(kron_ref, 2 * j, w_left, w_right)
         paired(j, 2 * j, x2_ref, x2t_ref, 2 * j)
+
+    mix = jnp.full((D, DD), math.tanh(FIELD), BF16)
+    for i in range(cols):
+        for d in range(0, DD, D):
+            a0, a1 = (x_ref[i, s, d : d + D] for s in range(2))
+            ax_ref[i, 0, d : d + D] = a0 + mix * a1
+            ax_ref[i, 1, d : d + D] = a1 + mix * a0
 
     n_rows = rows_arrive(rows_0, up_0, down_0, edge_rows)
     v_rows = rounded(n_rows[0])
@@ -610,19 +647,24 @@
         pltpu.make_async_copy(out_ref.at[i], out_hbm.at[i], store_sem.at[i]) for i in range(cols)
     ]
 
-    def gate(i):
-        gated = []
+    for i in range(cols):
         for s in range(2):
             left = by_major(late[s], 2 * cols) if i == 0 else by_major(early[s], i)
             right = (
                 by_minor(late[s], 2 * cols + 1) if i == cols - 1 else by_minor(early[s], i + 1)
             )
             at = (i * 2 + s) * 2
-            build_kron(kron_ref, at, by_major(late[s], cols + i), right)
+            down = math.cosh(FIELD) * by_major(late[s], cols + i)
+            build_kron(kron_ref, at, down, right)
             build_kron(kron_ref, at + 1, left, by_minor(late[s], i))
-            half = dot_nt(ax_ref[i, s], kron_ref[at]).astype(BF16)
-            gated.append(dot(kron_ref[at + 1], half).astype(BF16))
-        return gated
+    gated = [
+        [dot_nt(ax_ref[i, s], kron_ref[(i * 2 + s) * 2]).astype(BF16) for s in range(2)]
+        for i in range(cols)
+    ]
+    gated = [
+        [dot(kron_ref[(i * 2 + s) * 2 + 1], gated[i][s]).astype(BF16) for s in range(2)]
+        for i in range(cols)
+    ]
 
     def emit(i, gated):
         for b in range(0, mixed, 2):
@@ -651,11 +693,8 @@
                     ]
         stores[i].start()
 
-    waiting = gate(0)
     for i in range(cols):
-        following = gate(i + 1) if i + 1 < cols else None
-        emit(i, waiting)
-        waiting = following
+        emit(i, gated[i])
     for store in stores + [store_msg]:
         store.wait()
 

time: 16.6 us -> 14.9 us (0.90)
  Pallas kernels: 15.8 us -> 14 us
    pallas_call x1, Pallas kernels: 12.7 us -> 11.4 us  [per_device(): pl.pallas_call(functools.partial(messages_kernel, tiles, groups, cols, D)...]
    pallas_call x1, Pallas kernels: 3.09 us -> 2.56 us  [per_device(): pl.pallas_call(functools.partial(gates_kernel, tiles, groups, cols, D), o...]
where the time goes in v5:
time: 14.9 us; the launch traced here: 14.6 us
  Pallas kernels  14 us (94%)
  between operations  0.64 us (4%)
    pallas_call x1, Pallas kernels, per_device(): pl.pallas_call(functools.partial(messages_kernel, tiles, groups, cols, D)...  11.4 us
    pallas_call x1, Pallas kernels, per_device(): pl.pallas_call(functools.partial(gates_kernel, tiles, groups, cols, D), o...  2.56 us

profile of v5, /device:TPU:0, one launch (start us, length us, event | category | flops | bytes accessed | tf_op | source)
XLA Modules:
  0.0 14.6 jit_solution(3346702166887495753)
XLA Ops:
  0.6 11.4 %shard_map.41 = (bf16[3,2,256,256]{3,2,1,0:T(8,128)(2,1)S(1)}, f32[2,16,128]{2,1,0:T(8,128)S(1)}, f32[2,16,128]{2,1,0:T(8,128)S(1)}, f32[2,16,128]{2,1,0:T(8,128)S(1)}) custom-call(bf16[3,1024,128]{2,1,0:T(8,128)(2,1)} %bitcast.12, f32[3,4,256]{2,1,0:T(4,128)} %bitcast.13), custom_call_target="tpu_custom_call" | custom-call | tf_op jit(solution)/shard_map/pallas_call | solution.py:711
  12.1 2.6 %shard_map.42 = (bf16[3,1024,128]{2,1,0:T(8,128)(2,1)}, f32[3,4,256]{2,1,0:T(4,128)}) custom-call(bf16[3,2,256,256]{3,2,1,0:T(8,128)(2,1)S(1)} %get-tuple-element.8.ax_ref, f32[2,16,128]{2,1,0:T(8,128)S(1)} %get-tuple-element.9.env_ref, f32[2,16,128]{2,1,0:T(8,128)S(1)} %get-tuple-element.10.inner_ref, f32[2,16,128]{2,1,0:T(8,128)S(1)} %get-tuple-element.11.in_ref), custom_call_target="tpu_custom_call" | custom-call | tf_op jit(solution)/shard_map/pallas_call | solution.py:746

commit v6 on v5

--- a/solution.py
+++ b/solution.py
@@ -142,7 +142,7 @@
 
 def messages_kernel(tiles, groups, cols, D, a_hbm, msg_hbm, ax_ref, env_ref, inner_ref, mout_ref,
            a_ref, msg_ref, x_ref, xt_ref, x2_ref, x2t_ref, kron_ref, gram_ref,
-           send_v0, send_v1, send_s0, send_s1, up_0, up_1, down_0, down_1, side_0, side_1,
+           send_v0, send_v1, send_s0, send_s1, _, send_f1, up_0, up_1, down_0, down_1, side_0, side_1,
            send_sem, recv_sem, load_sem):
     loads = [pltpu.make_async_copy(msg_hbm, msg_ref, load_sem.at[cols])]
     loads += [
@@ -281,42 +281,27 @@
             recv_sem=recv_sem.at[turn, k], device_id=device, device_id_type=MESH,
         )
 
-    def rows_copies(turn, src, up_dst, down_dst):
-        to_up = copy(src, down_dst, turn, 0, {"tile": tile - 1})
-        to_down = copy(src, up_dst, turn, 1, {"tile": tile + 1})
-
+    def above_arrives(sent, arriving, dst, edges):
         @pl.when(has_up)
         def _():
-            to_up.start()
-
+            sent.wait_send()
+            arriving.wait_recv()
+
+        @pl.when(jnp.logical_not(has_up))
+        def _():
+            dst[...] = edges
+
+    def below_arrives(sent, arriving, dst, edges):
         @pl.when(has_down)
         def _():
-            to_down.start()
-
-        return to_up, to_down
-
-    def rows_arrive(copies, up_dst, down_dst, edges):
-        to_up, to_down = copies
-
-        @pl.when(has_up)
-        def _():
-            to_up.wait_send()
-            to_down.wait_recv()
-
-        @pl.when(jnp.logical_not(has_up))
-        def _():
-            up_dst[...] = edges
-
-        @pl.when(has_down)
-        def _():
-            to_down.wait_send()
-            to_up.wait_recv()
+            sent.wait_send()
+            arriving.wait_recv()
 
         @pl.when(jnp.logical_not(has_down))
         def _():
-            down_dst[...] = edges
-
-        above, below = up_dst[...], down_dst[...]
+            dst[...] = edges
+
+    def joined_rows(above, below):
         return [
             jnp.where(slot < cols, above[k * D : (k + 1) * D], below[k * D : (k + 1) * D])
             for k in range(above.shape[0] // D)
@@ -434,12 +419,13 @@
         for s in range(2):
             xt_ref[i, s] = x_ref[i, s].T
     sides_of = ((x_ref, xt_ref), (xt_ref, x_ref))
-    for path, (left, right) in enumerate(sides_of):
-        for i in range(cols):
-            y = [dot(left[i, s], kron_ref[2 * i + path]).astype(BF16) for s in range(2)]
-            gram_ref[2 * i + path, 0] = dot(
-                jnp.concatenate(y, axis=1), right[i].reshape(2 * DD, DD)
-            )
+
+    def first_gram(path, i):
+        left, right = sides_of[path]
+        y = [dot(left[i, s], kron_ref[2 * i + path]).astype(BF16) for s in range(2)]
+        gram_ref[2 * i + path, 0] = dot(
+            jnp.concatenate(y, axis=1), right[i].reshape(2 * DD, DD)
+        )
 
     def outer(i, leg):
         w_up, w_down, w_left, w_right = weights[i]
@@ -451,12 +437,15 @@
             return [reduce_minor(gram_ref[2 * i + 1, 0], w_right)]
         return [reduce_major(gram_ref[2 * i + 1, 0], w_down)]
 
-    first_minors = minors([outer(i, 0) for i in range(cols)] + [outer(cols - 1, 3)])
-    first_majors = majors([outer(i, 2) for i in range(cols)] + [outer(0, 1)])
-    ups, right_last = first_minors[:cols], first_minors[cols]
-    downs, left_first = first_majors[:cols], first_majors[cols]
-    send_v0[...] = normalised([upright(downs, ups, 0)])[0]
+    first_gram(0, 0)
+    first_gram(1, cols - 1)
+    for i in range(1, cols):
+        first_gram(0, i)
+    for i in range(cols - 1):
+        first_gram(1, i)
+    (left_first,), (right_last,) = majors([outer(0, 1)]), minors([outer(cols - 1, 3)])
     send_s0[...] = normalised([jnp.where(from_left, right_last[0], left_first[0])])[0]
+    ups = [outer(i, 0) for i in range(cols)]
 
     inside = jnp.logical_and(has_up, has_down)
 
@@ -468,9 +457,21 @@
     def _():
         pl.semaphore_wait(barrier, 2)
 
-    rows_0 = rows_copies(0, send_v0, up_0, down_0)
     sides_0 = copy(send_s0, side_0, 0, 2, {"group": 1 - group})
     sides_0.start()
+    downs = majors([outer(i, 2) for i in range(cols)])
+    ups = minors(ups)
+    send_v0[...] = normalised([upright(downs, ups, 0)])[0]
+    to_up = copy(send_v0, down_0, 0, 0, {"tile": tile - 1})
+    to_down = copy(send_v0, up_0, 0, 1, {"tile": tile + 1})
+
+    @pl.when(has_up)
+    def _():
+        to_up.start()
+
+    @pl.when(has_down)
+    def _():
+        to_down.start()
 
     for i in range(cols):
         for s in range(2):
@@ -514,16 +515,26 @@
             ax_ref[i, 0, d : d + D] = a0 + mix * a1
             ax_ref[i, 1, d : d + D] = a1 + mix * a0
 
-    n_rows = rows_arrive(rows_0, up_0, down_0, edge_rows)
-    v_rows = rounded(n_rows[0])
-    ups, downs, weights = [], [], []
-    for j in range(cols):
-        i = order[j]
-        w_up, w_down = by_minor(v_rows, i), by_major(v_rows, cols + i)
-        weights.append((w_up, w_down))
-        ups.append(kinds_of([reduce_major(gram_ref[2 * j, s], w_down) for s in range(2)]))
-        downs.append(kinds_of([reduce_minor(gram_ref[2 * j, s], w_up) for s in range(2)]))
-    ups, downs = minors(ups), majors(downs)
+    far_up = lax.rem(tile, 2) == 0
+    far_down = jnp.logical_not(far_up)
+
+    def above_0():
+        above_arrives(to_up, to_down, up_0, edge_rows)
+
+    def below_0():
+        below_arrives(to_down, to_up, down_0, edge_rows)
+
+    def up_legs(rows, j):
+        weight = by_major(rows, cols + order[j])
+        return kinds_of([reduce_major(gram_ref[2 * j, s], weight) for s in range(2)])
+
+    def down_legs(rows, j):
+        weight = by_minor(rows, order[j])
+        return kinds_of([reduce_minor(gram_ref[2 * j, s], weight) for s in range(2)])
+
+    def ship(buffer, values):
+        for k in range(2):
+            buffer[k * D : (k + 1) * D] = values[k]
 
     def ordered(above, below, kind):
         return placed(
@@ -531,11 +542,47 @@
             + [(cols + order[j], below[j][kind]) for j in range(cols)]
         )
 
-    out_rows = normalised([ordered(downs, ups, k) for k in range(2)])
-    for k in range(2):
-        send_v1[k * D : (k + 1) * D] = out_rows[k]
-    rows_1 = rows_copies(1, send_v1, up_1, down_1)
-    o_rows = normalised([ordered(ups, downs, k) for k in range(2)])
+    nothing = [[jnp.zeros((D, LANES), F32)] * 2] * cols
+    up_far = copy(send_f1, down_1, 1, 0, {"tile": tile - 1})
+    up_near = copy(send_v1, down_1, 1, 0, {"tile": tile - 1})
+    down_far = copy(send_f1, up_1, 1, 1, {"tile": tile + 1})
+    down_near = copy(send_v1, up_1, 1, 1, {"tile": tile + 1})
+
+    @pl.when(far_up)
+    def _():
+        below_0()
+        rows = rounded(down_0[...])
+        legs_up = minors([up_legs(rows, j) for j in range(cols)])
+        ship(send_f1, normalised([ordered(nothing, legs_up, k) for k in range(2)]))
+
+        @pl.when(has_up)
+        def _():
+            up_far.start()
+
+    @pl.when(far_down)
+    def _():
+        above_0()
+        rows = rounded(up_0[...])
+        legs_down = majors([down_legs(rows, j) for j in range(cols)])
+        ship(send_f1, normalised([ordered(legs_down, nothing, k) for k in range(2)]))
+
+        @pl.when(has_down)
+        def _():
+            down_far.start()
+
+    @pl.when(far_up)
+    def _():
+        above_0()
+
+    @pl.when(far_down)
+    def _():
+        below_0()
+
+    v_rows = rounded(joined_rows(up_0[...], down_0[...])[0])
+    weights = []
+    for j in range(cols):
+        i = order[j]
+        weights.append((by_minor(v_rows, i), by_major(v_rows, cols + i)))
 
     def horizontal(j):
         build_kron(kron_ref, 2 * j + 1, weights[j][1], weights[j][0])
@@ -547,11 +594,30 @@
 
     left, right = horizontal(cols - 1)
     (left,), (right,) = majors([left]), minors([right])
-    out_sides = normalised([jnp.where(from_left, right[k], left[k]) for k in range(2)])
-    for k in range(2):
-        send_s1[k * D : (k + 1) * D] = out_sides[k]
+    ship(send_s1, normalised([jnp.where(from_left, right[k], left[k]) for k in range(2)]))
     sides_1 = copy(send_s1, side_1, 1, 2, {"group": 1 - group})
-    sides_1.start()
+
+    @pl.when(far_up)
+    def _():
+        sides_1.start()
+
+    @pl.when(far_down)
+    def _():
+        sides_1.start()
+
+    ups = minors([up_legs(v_rows, j) for j in range(cols)])
+    downs = majors([down_legs(v_rows, j) for j in range(cols)])
+    ship(send_v1, normalised([ordered(downs, ups, k) for k in range(2)]))
+
+    @pl.when(far_up & has_down)
+    def _():
+        down_near.start()
+
+    @pl.when(far_down & has_up)
+    def _():
+        up_near.start()
+
+    o_rows = normalised([ordered(ups, downs, k) for k in range(2)])
     others = [horizontal(j) for j in range(cols - 1)]
     lefts = majors([o[0] for o in others]) + [left]
     rights = minors([o[1] for o in others]) + [right]
@@ -577,7 +643,10 @@
         inner_ref[s] = rounded(weight)
     zero = jnp.zeros((D, LANES), F32)
     n_sides = sides_arrive(sides_1, side_1, n_sides, [edge_sides, zero])
-    n_rows = rows_arrive(rows_1, up_1, down_1, jnp.concatenate([edge_rows, zero], axis=0))
+    rows_edges = jnp.concatenate([edge_rows, zero], axis=0)
+    above_arrives(up_near, down_near, up_1, rows_edges)
+    below_arrives(down_near, up_near, down_1, rows_edges)
+    n_rows = joined_rows(up_1[...], down_1[...])
     for k in range(2):
         env_ref[k] = jnp.where(
             slot < 2 * cols, o_rows[k] + n_rows[k], o_sides[k] + n_sides[k]
@@ -729,7 +798,7 @@
             pltpu.VMEM((2 * cols, 2, DD, DD), F32),
         ]
         + [
-            pltpu.VMEM(((1 + turn) * D, LANES), F32) for _ in range(5) for turn in range(ITERS)
+            pltpu.VMEM(((1 + turn) * D, LANES), F32) for _ in range(6) for turn in range(ITERS)
         ]
         + [
             pltpu.SemaphoreType.DMA((ITERS, 3)),

time: 14.9 us -> 14.7 us (0.987)
  no operation moved by 1% of the time
where the time goes in v6:
time: 14.7 us; the launch traced here: 14.5 us
  Pallas kernels  13.9 us (95%)
  between operations  0.64 us (4%)
    pallas_call x1, Pallas kernels, per_device(): pl.pallas_call(functools.partial(messages_kernel, tiles, groups, cols, D)...  11.3 us
    pallas_call x1, Pallas kernels, per_device(): pl.pallas_call(functools.partial(gates_kernel, tiles, groups, cols, D), o...  2.56 us

profile of v6, /device:TPU:0, one launch (start us, length us, event | category | flops | bytes accessed | tf_op | source)
XLA Modules:
  0.0 14.5 jit_solution(10353971233389652890)
XLA Ops:
  0.6 11.3 %shard_map.41 = (bf16[3,2,256,256]{3,2,1,0:T(8,128)(2,1)S(1)}, f32[2,16,128]{2,1,0:T(8,128)S(1)}, f32[2,16,128]{2,1,0:T(8,128)S(1)}, f32[2,16,128]{2,1,0:T(8,128)S(1)}) custom-call(bf16[3,1024,128]{2,1,0:T(8,128)(2,1)} %bitcast.12, f32[3,4,256]{2,1,0:T(4,128)} %bitcast.13), custom_call_target="tpu_custom_call" | custom-call | tf_op jit(solution)/shard_map/pallas_call | solution.py:780
  11.9 2.6 %shard_map.42 = (bf16[3,1024,128]{2,1,0:T(8,128)(2,1)}, f32[3,4,256]{2,1,0:T(4,128)}) custom-call(bf16[3,2,256,256]{3,2,1,0:T(8,128)(2,1)S(1)} %get-tuple-element.8.ax_ref, f32[2,16,128]{2,1,0:T(8,128)S(1)} %get-tuple-element.9.env_ref, f32[2,16,128]{2,1,0:T(8,128)S(1)} %get-tuple-element.10.inner_ref, f32[2,16,128]{2,1,0:T(8,128)S(1)} %get-tuple-element.11.in_ref), custom_call_target="tpu_custom_call" | custom-call | tf_op jit(solution)/shard_map/pallas_call | solution.py:815

commit v7 on v6

--- a/solution.py
+++ b/solution.py
@@ -141,7 +141,7 @@
 
 
 def messages_kernel(tiles, groups, cols, D, a_hbm, msg_hbm, ax_ref, env_ref, inner_ref, mout_ref,
-           a_ref, msg_ref, x_ref, xt_ref, x2_ref, x2t_ref, kron_ref, gram_ref,
+           a_ref, msg_ref, near_ref, x_ref, xt_ref, x2_ref, x2t_ref, kron_ref, gram_ref,
            send_v0, send_v1, send_s0, send_s1, _, send_f1, up_0, up_1, down_0, down_1, side_0, side_1,
            send_sem, recv_sem, load_sem):
     loads = [pltpu.make_async_copy(msg_hbm, msg_ref, load_sem.at[cols])]
@@ -447,6 +447,13 @@
     send_s0[...] = normalised([jnp.where(from_left, right_last[0], left_first[0])])[0]
     ups = [outer(i, 0) for i in range(cols)]
 
+    mix = jnp.full((D, DD), math.tanh(FIELD), BF16)
+    for i in range(cols):
+        for d in range(0, DD, D):
+            a0, a1 = (x_ref[i, s, d : d + D] for s in range(2))
+            ax_ref[i, 0, d : d + D] = a0 + mix * a1
+            ax_ref[i, 1, d : d + D] = a1 + mix * a0
+
     inside = jnp.logical_and(has_up, has_down)
 
     @pl.when(inside)
@@ -488,6 +495,15 @@
 
     n_sides = normalised([inner_view(lefts, rights, 0)])
 
+    far_up = lax.rem(tile, 2) == 0
+    far_down = jnp.logical_not(far_up)
+
+    def above_0():
+        above_arrives(to_up, to_down, up_0, edge_rows)
+
+    def below_0():
+        below_arrives(to_down, to_up, down_0, edge_rows)
+
     side_weights = []
 
     def paired(j, kron, left, right, at):
@@ -498,7 +514,22 @@
 
     for j in range(cols):
         if j == cols - 1:
+            @pl.when(far_up)
+            def _():
+                below_0()
+                near_ref[...] = down_0[...]
+
+            @pl.when(far_down)
+            def _():
+                above_0()
+                near_ref[...] = up_0[...]
+
             n_sides = sides_arrive(sides_0, side_0, n_sides, [edge_sides])
+            near_rows = rounded(near_ref[...])
+            near_weights = [
+                (by_minor(near_rows, order[n]), by_major(near_rows, cols + order[n]))
+                for n in range(cols)
+            ]
         v_sides = rounded(n_sides[0]) if j == cols - 1 else rounded(jnp.where(
             from_left | from_right, edge_sides, n_sides[0]
         ))
@@ -508,28 +539,10 @@
         build_kron(kron_ref, 2 * j, w_left, w_right)
         paired(j, 2 * j, x2_ref, x2t_ref, 2 * j)
 
-    mix = jnp.full((D, DD), math.tanh(FIELD), BF16)
-    for i in range(cols):
-        for d in range(0, DD, D):
-            a0, a1 = (x_ref[i, s, d : d + D] for s in range(2))
-            ax_ref[i, 0, d : d + D] = a0 + mix * a1
-            ax_ref[i, 1, d : d + D] = a1 + mix * a0
-
-    far_up = lax.rem(tile, 2) == 0
-    far_down = jnp.logical_not(far_up)
-
-    def above_0():
-        above_arrives(to_up, to_down, up_0, edge_rows)
-
-    def below_0():
-        below_arrives(to_down, to_up, down_0, edge_rows)
-
-    def up_legs(rows, j):
-        weight = by_major(rows, cols + order[j])
+    def up_legs(weight, j):
         return kinds_of([reduce_major(gram_ref[2 * j, s], weight) for s in range(2)])
 
-    def down_legs(rows, j):
-        weight = by_minor(rows, order[j])
+    def down_legs(weight, j):
         return kinds_of([reduce_minor(gram_ref[2 * j, s], weight) for s in range(2)])
 
     def ship(buffer, values):
@@ -550,9 +563,7 @@
 
     @pl.when(far_up)
     def _():
-        below_0()
-        rows = rounded(down_0[...])
-        legs_up = minors([up_legs(rows, j) for j in range(cols)])
+        legs_up = minors([up_legs(near_weights[j][1], j) for j in range(cols)])
         ship(send_f1, normalised([ordered(nothing, legs_up, k) for k in range(2)]))
 
         @pl.when(has_up)
@@ -561,9 +572,7 @@
 
     @pl.when(far_down)
     def _():
-        above_0()
-        rows = rounded(up_0[...])
-        legs_down = majors([down_legs(rows, j) for j in range(cols)])
+        legs_down = majors([down_legs(near_weights[j][0], j) for j in range(cols)])
         ship(send_f1, normalised([ordered(legs_down, nothing, k) for k in range(2)]))
 
         @pl.when(has_down)
@@ -584,40 +593,52 @@
         i = order[j]
         weights.append((by_minor(v_rows, i), by_major(v_rows, cols + i)))
 
-    def horizontal(j):
+    def horizontal_gram(j):
         build_kron(kron_ref, 2 * j + 1, weights[j][1], weights[j][0])
         paired(j, 2 * j + 1, x2t_ref, x2_ref, 2 * j + 1)
+
+    def horizontal(j):
         w_left, w_right = side_weights[j]
         left = kinds_of([reduce_minor(gram_ref[2 * j + 1, s], w_right) for s in range(2)])
         right = kinds_of([reduce_major(gram_ref[2 * j + 1, s], w_left) for s in range(2)])
         return left, right
 
+    horizontal_gram(cols - 1)
     left, right = horizontal(cols - 1)
     (left,), (right,) = majors([left]), minors([right])
     ship(send_s1, normalised([jnp.where(from_left, right[k], left[k]) for k in range(2)]))
     sides_1 = copy(send_s1, side_1, 1, 2, {"group": 1 - group})
-
+    sides_1.start()
     @pl.when(far_up)
     def _():
-        sides_1.start()
+        for j in range(cols - 1):
+            horizontal_gram(j)
+        near = majors([down_legs(weights[j][0], j) for j in range(cols)])
+        ship(send_v1, normalised([ordered(near, nothing, k) for k in range(2)]))
+
+        @pl.when(has_down)
+        def _():
+            down_near.start()
 
     @pl.when(far_down)
     def _():
-        sides_1.start()
-
-    ups = minors([up_legs(v_rows, j) for j in range(cols)])
-    downs = majors([down_legs(v_rows, j) for j in range(cols)])
-    ship(send_v1, normalised([ordered(downs, ups, k) for k in range(2)]))
-
-    @pl.when(far_up & has_down)
-    def _():
-        down_near.start()
-
-    @pl.when(far_down & has_up)
-    def _():
-        up_near.start()
-
-    o_rows = normalised([ordered(ups, downs, k) for k in range(2)])
+        for j in range(cols - 1):
+            horizontal_gram(j)
+        near = minors([up_legs(weights[j][1], j) for j in range(cols)])
+        ship(send_v1, normalised([ordered(nothing, near, k) for k in range(2)]))
+
+        @pl.when(has_up)
+        def _():
+            up_near.start()
+
+    half = cols * D
+    swapped = jnp.where(
+        slot < cols, lane + half, jnp.where(slot < 2 * cols, lane - half, lane)
+    )
+    o_rows = [
+        pick(send_f1[k * D : (k + 1) * D] + send_v1[k * D : (k + 1) * D], swapped)
+        for k in range(2)
+    ]
     others = [horizontal(j) for j in range(cols - 1)]
     lefts = majors([o[0] for o in others]) + [left]
     rights = minors([o[1] for o in others]) + [right]
@@ -790,6 +811,7 @@
         scratch_shapes=[
             pltpu.VMEM(a.shape, BF16),
             pltpu.VMEM((cols, 4, DD), F32),
+            pltpu.VMEM((D, LANES), F32),
             pltpu.VMEM((cols, 2, DD, DD), BF16),
             pltpu.VMEM((cols, 2, DD, DD), BF16),
             pltpu.VMEM((cols, 2, DD, DD), BF16),

time: 14.7 us -> 14.5 us (0.986)
  Pallas kernels: 13.9 us -> 13.7 us
    pallas_call x1, Pallas kernels: 11.3 us -> 11.1 us  [per_device(): pl.pallas_call(functools.partial(messages_kernel, tiles, groups, cols, D)...]
where the time goes in v7:
time: 14.5 us; the launch traced here: 14.3 us
  Pallas kernels  13.7 us (94%)
  between operations  0.64 us (4%)
    pallas_call x1, Pallas kernels, per_device(): pl.pallas_call(functools.partial(messages_kernel, tiles, groups, cols, D)...  11.1 us
    pallas_call x1, Pallas kernels, per_device(): pl.pallas_call(functools.partial(gates_kernel, tiles, groups, cols, D), o...  2.56 us

profile of v7, /device:TPU:0, one launch (start us, length us, event | category | flops | bytes accessed | tf_op | source)
XLA Modules:
  0.0 14.3 jit_solution(10759597450726382570)
XLA Ops:
  0.6 11.1 %shard_map.41 = (bf16[3,2,256,256]{3,2,1,0:T(8,128)(2,1)S(1)}, f32[2,16,128]{2,1,0:T(8,128)S(1)}, f32[2,16,128]{2,1,0:T(8,128)S(1)}, f32[2,16,128]{2,1,0:T(8,128)S(1)}) custom-call(bf16[3,1024,128]{2,1,0:T(8,128)(2,1)} %bitcast.12, f32[3,4,256]{2,1,0:T(4,128)} %bitcast.13), custom_call_target="tpu_custom_call" | custom-call | tf_op jit(solution)/shard_map/pallas_call | solution.py:801
  11.7 2.6 %shard_map.42 = (bf16[3,1024,128]{2,1,0:T(8,128)(2,1)}, f32[3,4,256]{2,1,0:T(4,128)}) custom-call(bf16[3,2,256,256]{3,2,1,0:T(8,128)(2,1)S(1)} %get-tuple-element.8.ax_ref, f32[2,16,128]{2,1,0:T(8,128)S(1)} %get-tuple-element.9.env_ref, f32[2,16,128]{2,1,0:T(8,128)S(1)} %get-tuple-element.10.inner_ref, f32[2,16,128]{2,1,0:T(8,128)S(1)} %get-tuple-element.11.in_ref), custom_call_target="tpu_custom_call" | custom-call | tf_op jit(solution)/shard_map/pallas_call | solution.py:837

commit v8 on v7

--- a/solution.py
+++ b/solution.py
@@ -10,6 +10,7 @@
 
 ITERS = 2
 NS_STEPS = 6
+EARLY_STEPS = 3
 LANES = 128
 EPSILON = 1e-06
 COUPLING = 0.5
@@ -70,14 +71,12 @@
     return jnp.broadcast_to(value[k : k + 1, :], value.shape)
 
 
-def bond_weights(msg_sum, twist_sum):
+def bond_open(msg_sum, twist_sum):
     D = msg_sum.shape[0]
     lane = iota((D, LANES), 1)
     row = iota((D, LANES), 0)
     inner = lane & (D - 1)
-    start = lane - inner
-    turned = start + row
-    unit = jnp.where(inner == row, 1.0, 0.0).astype(F32)
+    turned = lane - inner + row
     g0, g1 = math.cosh(COUPLING), math.sinh(COUPLING)
     cross = math.sqrt(g0 * g1)
     root2 = math.sqrt(2.0)
@@ -102,6 +101,16 @@
             transposed = placed if transposed is None else transposed + placed
         rotated.append(transposed)
 
+    return gram / trace, rotated, jnp.broadcast_to(trace, (D, LANES))
+
+
+def bond_tools(D):
+    lane = iota((D, LANES), 1)
+    row = iota((D, LANES), 0)
+    inner = lane & (D - 1)
+    turned = lane - inner + row
+    unit = jnp.where(inner == row, 1.0, 0.0).astype(F32)
+
     def columns(value):
         return [pick(row_of(value, k), turned) for k in range(D)]
 
@@ -112,12 +121,20 @@
             sums[k % 4] = term if sums[k % 4] is None else sums[k % 4] + term
         return (sums[0] + sums[1]) + (sums[2] + sums[3])
 
-    state = gram / trace
-    for step in range(NS_STEPS - 2):
-        left = columns(state)
-        square = times(left, state)
-        rotated = [1.5 * v - 0.5 * times(left, v) for v in rotated]
-        state = times(left, 2.25 * unit - 1.5 * state + 0.25 * square)
+    return unit, columns, times
+
+
+def bond_step(state, rotated):
+    unit, columns, times = bond_tools(state.shape[0])
+    left = columns(state)
+    square = times(left, state)
+    rotated = [1.5 * v - 0.5 * times(left, v) for v in rotated]
+    state = times(left, 2.25 * unit - 1.5 * state + 0.25 * square)
+    return state, rotated
+
+
+def bond_close(state, rotated, trace):
+    _, columns, times = bond_tools(state.shape[0])
     left = columns(state)
     rotated = [1.5 * v - 0.5 * times(left, v) for v in rotated]
     again = rotated
@@ -125,8 +142,8 @@
         again = [1.5 * v - 0.5 * times(left, v) for v in again]
     rotated = [1.5 * v - 0.5 * times(left, w) for v, w in zip(rotated, again)]
     scale = 1.0 / jnp.sqrt(trace)
-    first = math.sqrt(g0) * rotated[0] * scale
-    second = math.sqrt(g1) * rotated[1] * scale
+    first = math.sqrt(math.cosh(COUPLING)) * rotated[0] * scale
+    second = math.sqrt(math.sinh(COUPLING)) * rotated[1] * scale
     return [first + second, first - second]
 
 
@@ -660,8 +677,11 @@
 
     o_sides = normalised([own_sides(k) for k in range(2)])
     n_sides = normalised([other_sides(k) for k in range(2)])
-    for s, weight in enumerate(bond_weights(*[o + n for o, n in zip(o_sides, n_sides)])):
-        inner_ref[s] = rounded(weight)
+    state, rotated, trace = bond_open(*[o + n for o, n in zip(o_sides, n_sides)])
+    for step in range(EARLY_STEPS):
+        state, rotated = bond_step(state, rotated)
+    for n, value in enumerate([state] + rotated + [trace]):
+        inner_ref[n] = value
     zero = jnp.zeros((D, LANES), F32)
     n_sides = sides_arrive(sides_1, side_1, n_sides, [edge_sides, zero])
     rows_edges = jnp.concatenate([edge_rows, zero], axis=0)
@@ -698,11 +718,21 @@
         | ((slot == 2 * cols) & (group == 0))
         | ((slot == 2 * cols + 1) & (group == groups - 1))
     )
+    state, rotated, trace = bond_open(env_ref[0], env_ref[1])
+    begun, turning = inner_ref[0], [inner_ref[1], inner_ref[2]]
+    early_left = NS_STEPS - 2 - EARLY_STEPS
+    for step in range(NS_STEPS - 2):
+        if step < early_left:
+            begun, turning = bond_step(begun, turning)
+        elif step == early_left:
+            early = [
+                w.astype(BF16).astype(F32) for w in bond_close(begun, turning, inner_ref[3])
+            ]
+        state, rotated = bond_step(state, rotated)
     late = [
         jnp.where(at_edge, unit, w).astype(BF16).astype(F32)
-        for w in bond_weights(env_ref[0], env_ref[1])
+        for w in bond_close(state, rotated, trace)
     ]
-    early = [inner_ref[s] for s in range(2)]
 
     unfold_mask = slot == (row & (LANES // D - 1))
     flat_rows = []
@@ -803,7 +833,7 @@
         out_shape=(
             jax.ShapeDtypeStruct((cols, 2, DD, DD), BF16),
             jax.ShapeDtypeStruct((2, D, LANES), F32),
-            jax.ShapeDtypeStruct((2, D, LANES), F32),
+            jax.ShapeDtypeStruct((4, D, LANES), F32),
             jax.ShapeDtypeStruct((2, D, LANES), F32),
         ),
         in_specs=[hbm, hbm],

time: 14.5 us -> 14.5 us (level)
    pallas_call x1, Pallas kernels: 11.1 us -> 10.9 us  [per_device(): pl.pallas_call(functools.partial(messages_kernel, tiles, groups, cols, D)...]
where the time goes in v8:
time: 14.5 us; the launch traced here: 14.2 us
  Pallas kernels  13.6 us (94%)
  between operations  0.64 us (4%)
    pallas_call x1, Pallas kernels, per_device(): pl.pallas_call(functools.partial(messages_kernel, tiles, groups, cols, D)...  10.9 us
    pallas_call x1, Pallas kernels, per_device(): pl.pallas_call(functools.partial(gates_kernel, tiles, groups, cols, D), o...  2.67 us

profile of v8, /device:TPU:0, one launch (start us, length us, event | category | flops | bytes accessed | tf_op | source)
XLA Modules:
  0.0 14.2 jit_solution(1312810266873821603)
XLA Ops:
  0.6 10.9 %shard_map.41 = (bf16[3,2,256,256]{3,2,1,0:T(8,128)(2,1)S(1)}, f32[2,16,128]{2,1,0:T(8,128)S(1)}, f32[4,16,128]{2,1,0:T(8,128)S(1)}, f32[2,16,128]{2,1,0:T(8,128)S(1)}) custom-call(bf16[3,1024,128]{2,1,0:T(8,128)(2,1)} %bitcast.12, f32[3,4,256]{2,1,0:T(4,128)} %bitcast.13), custom_call_target="tpu_custom_call" | custom-call | tf_op jit(solution)/shard_map/pallas_call | solution.py:831
  11.6 2.7 %shard_map.42 = (bf16[3,1024,128]{2,1,0:T(8,128)(2,1)}, f32[3,4,256]{2,1,0:T(4,128)}) custom-call(bf16[3,2,256,256]{3,2,1,0:T(8,128)(2,1)S(1)} %get-tuple-element.8.ax_ref, f32[2,16,128]{2,1,0:T(8,128)S(1)} %get-tuple-element.9.env_ref, f32[4,16,128]{2,1,0:T(8,128)S(1)} %get-tuple-element.10.inner_ref, f32[2,16,128]{2,1,0:T(8,128)S(1)} %get-tuple-element.11.in_ref), custom_call_target="tpu_custom_call" | custom-call | tf_op jit(solution)/shard_map/pallas_call | solution.py:867

commit v9 on v8

--- a/solution.py
+++ b/solution.py
@@ -158,7 +158,7 @@
 
 
 def messages_kernel(tiles, groups, cols, D, a_hbm, msg_hbm, ax_ref, env_ref, inner_ref, mout_ref,
-           a_ref, msg_ref, near_ref, x_ref, xt_ref, x2_ref, x2t_ref, kron_ref, gram_ref,
+           a_ref, msg_ref, other_ref, x_ref, xt_ref, xq_ref, x2_ref, x2t_ref, kron_ref, gram_ref,
            send_v0, send_v1, send_s0, send_s1, _, send_f1, up_0, up_1, down_0, down_1, side_0, side_1,
            send_sem, recv_sem, load_sem):
     loads = [pltpu.make_async_copy(msg_hbm, msg_ref, load_sem.at[cols])]
@@ -181,6 +181,12 @@
     order = list(range(1, cols - 1)) + [closed, crossing]
     has_up = tile > 0
     has_down = tile < tiles - 1
+    far_path = lax.rem(tile, 2)
+    far_up = far_path == 0
+    far_down = jnp.logical_not(far_up)
+    swap_sides = far_path == group
+    cross_slot = jnp.where(group == 0, cols + crossing, crossing)
+    other_slot = jnp.where(group == 0, crossing, cols + crossing)
 
     barrier = pltpu.get_barrier_semaphore()
 
@@ -327,8 +333,7 @@
     from_left = (slot == 0) | (slot == 2 * cols)
     from_right = (slot == 2 * cols - 1) | (slot == 2 * cols + 1)
 
-    def sides_arrive(to_side, dst, local, edges):
-        to_side.wait()
+    def joined_sides(dst, local, edges):
         got = dst[...]
         out = []
         for k, (value, edge) in enumerate(zip(local, edges)):
@@ -389,36 +394,57 @@
                         (g // 2) * LANES : (g // 2 + 1) * LANES,
                     ] = block[g * span : (g + 1) * span, c * LANES : (c + 1) * LANES]
 
-    def relayout(i, s):
+    def exchanged(values, masks, unit_lanes):
+        step = 1
+        for high in masks:
+            out = list(values)
+            for a in range(len(values)):
+                if a & step:
+                    continue
+                b = a | step
+                low_up = pltpu.roll(values[b], unit_lanes * step, 1)
+                high_down = pltpu.roll(values[a], LANES - unit_lanes * step, 1)
+                out[a] = jnp.where(high[0], low_up, values[a])
+                out[b] = jnp.where(high[1], values[b], high_down)
+            values = out
+            step *= 2
+        return values
+
+    def relayout(j, s):
+        bits = per.bit_length() - 1
+        masks = [((slot & (1 << n)) != 0,) * 2 for n in range(bits)]
         for h in range(halves):
             for lh in range(halves):
                 values = [
                     x_ref[
-                        i, s, (lh * per + k) * D : (lh * per + k + 1) * D,
+                        order[j], s, (lh * per + k) * D : (lh * per + k + 1) * D,
                         h * LANES : (h + 1) * LANES,
                     ]
                     for k in range(per)
                 ]
-                step = 1
-                while step < per:
-                    high = (slot & step) != 0
-                    out = list(values)
-                    for a in range(per):
-                        if a & step:
-                            continue
-                        b = a | step
-                        low_up = pltpu.roll(values[b], D * step, 1)
-                        high_down = pltpu.roll(values[a], LANES - D * step, 1)
-                        out[a] = jnp.where(high, low_up, values[a])
-                        out[b] = jnp.where(high, values[b], high_down)
-                    values = out
-                    step *= 2
+                values = exchanged(values, masks, D)
                 for d in range(per):
                     x2_ref[
-                        i, s, (h * per + d) * D : (h * per + d + 1) * D,
+                        j, s, (h * per + d) * D : (h * per + d + 1) * D,
                         lh * LANES : (lh + 1) * LANES,
                     ] = values[d]
-        x2t_ref[i, s] = x2_ref[i, s].T
+        x2t_ref[j, s] = x2_ref[j, s].T
+
+    def cross_layout(s):
+        shut = jnp.where(swap_sides, 0, 1)
+        masks = []
+        for n in range(shift):
+            bit = (lane >> n) & 1
+            masks.append(((bit & (1 - shut)) != 0, (bit | shut) != 0))
+        for h in range(halves):
+            values = [
+                x_ref[crossing, s, k * D : (k + 1) * D, h * LANES : (h + 1) * LANES]
+                for k in range(D)
+            ]
+            values = exchanged(values, masks, 1)
+            for k in range(D):
+                xq_ref[0, s, k * D : (k + 1) * D, h * LANES : (h + 1) * LANES] = values[k]
+        xq_ref[1, s] = xq_ref[0, s].T
 
     v_rows, v_sides = rounded(edge_rows), rounded(edge_sides)
     weights = []
@@ -497,9 +523,10 @@
     def _():
         to_down.start()
 
-    for i in range(cols):
-        for s in range(2):
-            relayout(i, s)
+    for s in range(2):
+        for j in range(cols - 1):
+            relayout(j, s)
+        cross_layout(s)
 
     lefts = [left_first] + majors([outer(i, 1) for i in range(1, cols)])
     rights = minors([outer(i, 3) for i in range(cols - 1)]) + [right_last]
@@ -512,9 +539,6 @@
 
     n_sides = normalised([inner_view(lefts, rights, 0)])
 
-    far_up = lax.rem(tile, 2) == 0
-    far_down = jnp.logical_not(far_up)
-
     def above_0():
         above_arrives(to_up, to_down, up_0, edge_rows)
 
@@ -524,37 +548,29 @@
     side_weights = []
 
     def paired(j, kron, left, right, at):
-        i = order[j]
         for s in range(2):
-            y = dot(left[i, s], kron_ref[kron]).astype(BF16)
-            gram_ref[at, s] = dot(y, right[i, s])
-
-    for j in range(cols):
-        if j == cols - 1:
-            @pl.when(far_up)
-            def _():
-                below_0()
-                near_ref[...] = down_0[...]
-
-            @pl.when(far_down)
-            def _():
-                above_0()
-                near_ref[...] = up_0[...]
-
-            n_sides = sides_arrive(sides_0, side_0, n_sides, [edge_sides])
-            near_rows = rounded(near_ref[...])
-            near_weights = [
-                (by_minor(near_rows, order[n]), by_major(near_rows, cols + order[n]))
-                for n in range(cols)
-            ]
-        v_sides = rounded(n_sides[0]) if j == cols - 1 else rounded(jnp.where(
-            from_left | from_right, edge_sides, n_sides[0]
-        ))
+            y = dot(left[j, s], kron_ref[kron]).astype(BF16)
+            gram_ref[at, s] = dot(y, right[j, s])
+
+    v_sides = rounded(jnp.where(from_left | from_right, edge_sides, n_sides[0]))
+    for j in range(cols - 1):
         i = order[j]
         w_left, w_right = by_major(v_sides, i), by_minor(v_sides, cols + i)
         side_weights.append((w_left, w_right))
         build_kron(kron_ref, 2 * j, w_left, w_right)
         paired(j, 2 * j, x2_ref, x2t_ref, 2 * j)
+    other_major, other_minor = by_major(v_sides, other_slot), by_minor(v_sides, other_slot)
+
+    final = 2 * (cols - 1)
+
+    def crossing_gram(first, second, path):
+        build_kron(kron_ref, final, first, second)
+        for s in range(2):
+            y = dot(xq_ref[path, s], kron_ref[final]).astype(BF16)
+            gram_ref[final, s] = dot(y, xq_ref[1 - path, s])
+
+    def all_sides():
+        return rounded(joined_sides(side_0, n_sides, [edge_sides])[0])
 
     def up_legs(weight, j):
         return kinds_of([reduce_major(gram_ref[2 * j, s], weight) for s in range(2)])
@@ -578,37 +594,65 @@
     down_far = copy(send_f1, up_1, 1, 1, {"tile": tile + 1})
     down_near = copy(send_v1, up_1, 1, 1, {"tile": tile + 1})
 
+    sides_1 = copy(send_s1, side_1, 1, 2, {"group": 1 - group})
+
+    def cross_major(at, weight):
+        return kinds_of([reduce_major(gram_ref[at, s], weight) for s in range(2)])
+
+    def cross_minor(at, weight):
+        return kinds_of([reduce_minor(gram_ref[at, s], weight) for s in range(2)])
+
     @pl.when(far_up)
     def _():
-        legs_up = minors([up_legs(near_weights[j][1], j) for j in range(cols)])
+        below_0()
+        near = rounded(down_0[...])
+        crossing_gram(by_major(near, cols + crossing), other_minor, 0)
+        early = [up_legs(by_major(near, cols + order[j]), j) for j in range(cols - 1)]
+        early = minors(early)
+        sides_0.wait()
+        weight = by_major(all_sides(), cross_slot)
+        legs_up = early + minors([cross_major(final, weight)])
         ship(send_f1, normalised([ordered(nothing, legs_up, k) for k in range(2)]))
 
         @pl.when(has_up)
         def _():
             up_far.start()
 
+        above_0()
+        weight = by_minor(rounded(up_0[...]), crossing)
+        (cross,) = majors([cross_minor(final, weight)])
+        ship(send_s1, normalised(cross))
+        sides_1.start()
+
     @pl.when(far_down)
     def _():
-        legs_down = majors([down_legs(near_weights[j][0], j) for j in range(cols)])
+        above_0()
+        near = rounded(up_0[...])
+        crossing_gram(other_major, by_minor(near, crossing), 1)
+        early = [down_legs(by_minor(near, order[j]), j) for j in range(cols - 1)]
+        early = majors(early)
+        sides_0.wait()
+        weight = by_minor(all_sides(), cross_slot)
+        legs_down = early + majors([cross_minor(final, weight)])
         ship(send_f1, normalised([ordered(legs_down, nothing, k) for k in range(2)]))
 
         @pl.when(has_down)
         def _():
             down_far.start()
 
-    @pl.when(far_up)
-    def _():
-        above_0()
-
-    @pl.when(far_down)
-    def _():
         below_0()
+        weight = by_major(rounded(down_0[...]), cols + crossing)
+        (cross,) = minors([cross_major(final, weight)])
+        ship(send_s1, normalised(cross))
+        sides_1.start()
 
     v_rows = rounded(joined_rows(up_0[...], down_0[...])[0])
     weights = []
     for j in range(cols):
         i = order[j]
         weights.append((by_minor(v_rows, i), by_major(v_rows, cols + i)))
+    v_sides = all_sides()
+    cross_first, cross_second = by_major(v_sides, cross_slot), by_minor(v_sides, cross_slot)
 
     def horizontal_gram(j):
         build_kron(kron_ref, 2 * j + 1, weights[j][1], weights[j][0])
@@ -620,18 +664,23 @@
         right = kinds_of([reduce_major(gram_ref[2 * j + 1, s], w_left) for s in range(2)])
         return left, right
 
-    horizontal_gram(cols - 1)
-    left, right = horizontal(cols - 1)
-    (left,), (right,) = majors([left]), minors([right])
-    ship(send_s1, normalised([jnp.where(from_left, right[k], left[k]) for k in range(2)]))
-    sides_1 = copy(send_s1, side_1, 1, 2, {"group": 1 - group})
-    sides_1.start()
+    def last_gram(first, second, path):
+        build_kron(kron_ref, final + 1, first, second)
+        for s in range(2):
+            y = dot(xq_ref[path, s], kron_ref[final + 1]).astype(BF16)
+            gram_ref[final + 1, s] = dot(y, xq_ref[1 - path, s])
+
     @pl.when(far_up)
     def _():
+        last_gram(cross_first, weights[-1][0], 1)
         for j in range(cols - 1):
             horizontal_gram(j)
-        near = majors([down_legs(weights[j][0], j) for j in range(cols)])
+        near = [down_legs(weights[j][0], j) for j in range(cols - 1)]
+        near = majors(near + [cross_minor(final + 1, other_minor)])
         ship(send_v1, normalised([ordered(near, nothing, k) for k in range(2)]))
+        (other,) = minors([cross_major(final + 1, weights[-1][1])])
+        for k in range(2):
+            other_ref[k] = other[k]
 
         @pl.when(has_down)
         def _():
@@ -639,10 +688,15 @@
 
     @pl.when(far_down)
     def _():
+        last_gram(weights[-1][1], cross_second, 0)
         for j in range(cols - 1):
             horizontal_gram(j)
-        near = minors([up_legs(weights[j][1], j) for j in range(cols)])
+        near = [up_legs(weights[j][1], j) for j in range(cols - 1)]
+        near = minors(near + [cross_major(final + 1, other_major)])
         ship(send_v1, normalised([ordered(nothing, near, k) for k in range(2)]))
+        (other,) = majors([cross_minor(final + 1, weights[-1][0])])
+        for k in range(2):
+            other_ref[k] = other[k]
 
         @pl.when(has_up)
         def _():
@@ -657,25 +711,30 @@
         for k in range(2)
     ]
     others = [horizontal(j) for j in range(cols - 1)]
-    lefts = majors([o[0] for o in others]) + [left]
-    rights = minors([o[1] for o in others]) + [right]
+    lefts = majors([o[0] for o in others])
+    rights = minors([o[1] for o in others])
 
     def own_sides(kind):
-        base = placed(
-            [(order[j], lefts[j][kind]) for j in range(cols)]
-            + [(cols + order[j], rights[j][kind]) for j in range(cols)]
+        return placed(
+            [(order[j], lefts[j][kind]) for j in range(cols - 1)]
+            + [(cols + order[j], rights[j][kind]) for j in range(cols - 1)]
+            + [(other_slot, other_ref[kind])]
         )
-        base = jnp.where((slot == 2 * cols) & (group == groups - 1), lefts[-1][kind], base)
-        return jnp.where((slot == 2 * cols + 1) & (group == 0), rights[-1][kind], base)
 
     def other_sides(kind):
         entries = []
-        for j, i in enumerate(order):
+        for j in range(cols - 1):
+            i = order[j]
             entries.append((jnp.where(i == 0, -1, cols + i - 1), lefts[j][kind]))
             entries.append((jnp.where(i == cols - 1, -1, i + 1), rights[j][kind]))
+        entries.append((jnp.where(group == 0, cols + crossing - 1, 1), other_ref[kind]))
         return placed(entries)
 
-    o_sides = normalised([own_sides(k) for k in range(2)])
+    is_cross = (slot == cross_slot) | (slot == jnp.where(group == 0, 2 * cols + 1, 2 * cols))
+    o_sides = [
+        jnp.where(is_cross, send_s1[k * D : (k + 1) * D], value)
+        for k, value in enumerate(normalised([own_sides(k) for k in range(2)]))
+    ]
     n_sides = normalised([other_sides(k) for k in range(2)])
     state, rotated, trace = bond_open(*[o + n for o, n in zip(o_sides, n_sides)])
     for step in range(EARLY_STEPS):
@@ -683,7 +742,8 @@
     for n, value in enumerate([state] + rotated + [trace]):
         inner_ref[n] = value
     zero = jnp.zeros((D, LANES), F32)
-    n_sides = sides_arrive(sides_1, side_1, n_sides, [edge_sides, zero])
+    sides_1.wait()
+    n_sides = joined_sides(side_1, n_sides, [edge_sides, zero])
     rows_edges = jnp.concatenate([edge_rows, zero], axis=0)
     above_arrives(up_near, down_near, up_1, rows_edges)
     below_arrives(down_near, up_near, down_1, rows_edges)
@@ -841,11 +901,12 @@
         scratch_shapes=[
             pltpu.VMEM(a.shape, BF16),
             pltpu.VMEM((cols, 4, DD), F32),
-            pltpu.VMEM((D, LANES), F32),
+            pltpu.VMEM((2, D, LANES), F32),
             pltpu.VMEM((cols, 2, DD, DD), BF16),
             pltpu.VMEM((cols, 2, DD, DD), BF16),
-            pltpu.VMEM((cols, 2, DD, DD), BF16),
-            pltpu.VMEM((cols, 2, DD, DD), BF16),
+            pltpu.VMEM((2, 2, DD, DD), BF16),
+            pltpu.VMEM((cols - 1, 2, DD, DD), BF16),
+            pltpu.VMEM((cols - 1, 2, DD, DD), BF16),
             pltpu.VMEM((2 * cols, DD, DD), BF16),
             pltpu.VMEM((2 * cols, 2, DD, DD), F32),
         ]

time: 14.5 us -> 14.2 us (0.979)
  Pallas kernels: 13.6 us -> 13.3 us
    pallas_call x1, Pallas kernels: 10.9 us -> 10.6 us  [per_device(): pl.pallas_call(functools.partial(messages_kernel, tiles, groups, cols, D)...]
where the time goes in v9:
time: 14.2 us; the launch traced here: 14 us
  Pallas kernels  13.3 us (94%)
  between operations  0.64 us (5%)
    pallas_call x1, Pallas kernels, per_device(): pl.pallas_call(functools.partial(messages_kernel, tiles, groups, cols, D)...  10.6 us
    pallas_call x1, Pallas kernels, per_device(): pl.pallas_call(functools.partial(gates_kernel, tiles, groups, cols, D), o...  2.67 us

profile of v9, /device:TPU:0, one launch (start us, length us, event | category | flops | bytes accessed | tf_op | source)
XLA Modules:
  0.0 14.0 jit_solution(7683771612632526926)
XLA Ops:
  0.6 10.6 %shard_map.41 = (bf16[3,2,256,256]{3,2,1,0:T(8,128)(2,1)S(1)}, f32[2,16,128]{2,1,0:T(8,128)S(1)}, f32[4,16,128]{2,1,0:T(8,128)S(1)}, f32[2,16,128]{2,1,0:T(8,128)S(1)}) custom-call(bf16[3,1024,128]{2,1,0:T(8,128)(2,1)} %bitcast.12, f32[3,4,256]{2,1,0:T(4,128)} %bitcast.13), custom_call_target="tpu_custom_call" | custom-call | tf_op jit(solution)/shard_map/pallas_call | solution.py:891
  11.3 2.7 %shard_map.42 = (bf16[3,1024,128]{2,1,0:T(8,128)(2,1)}, f32[3,4,256]{2,1,0:T(4,128)}) custom-call(bf16[3,2,256,256]{3,2,1,0:T(8,128)(2,1)S(1)} %get-tuple-element.8.ax_ref, f32[2,16,128]{2,1,0:T(8,128)S(1)} %get-tuple-element.9.env_ref, f32[4,16,128]{2,1,0:T(8,128)S(1)} %get-tuple-element.10.inner_ref, f32[2,16,128]{2,1,0:T(8,128)S(1)} %get-tuple-element.11.in_ref), custom_call_target="tpu_custom_call" | custom-call | tf_op jit(solution)/shard_map/pallas_call | solution.py:928

commit v10 on v9

--- a/solution.py
+++ b/solution.py
@@ -394,40 +394,45 @@
                         (g // 2) * LANES : (g // 2 + 1) * LANES,
                     ] = block[g * span : (g + 1) * span, c * LANES : (c + 1) * LANES]
 
-    def exchanged(values, masks, unit_lanes):
+    def exchanged(groups_of, masks, unit_lanes):
         step = 1
         for high in masks:
-            out = list(values)
-            for a in range(len(values)):
-                if a & step:
-                    continue
-                b = a | step
-                low_up = pltpu.roll(values[b], unit_lanes * step, 1)
-                high_down = pltpu.roll(values[a], LANES - unit_lanes * step, 1)
-                out[a] = jnp.where(high[0], low_up, values[a])
-                out[b] = jnp.where(high[1], values[b], high_down)
-            values = out
+            following = []
+            for values in groups_of:
+                out = list(values)
+                for a in range(len(values)):
+                    if a & step:
+                        continue
+                    b = a | step
+                    low_up = pltpu.roll(values[b], unit_lanes * step, 1)
+                    high_down = pltpu.roll(values[a], LANES - unit_lanes * step, 1)
+                    out[a] = jnp.where(high[0], low_up, values[a])
+                    out[b] = jnp.where(high[1], values[b], high_down)
+                following.append(out)
+            groups_of = following
             step *= 2
-        return values
+        return groups_of
 
     def relayout(j, s):
         bits = per.bit_length() - 1
         masks = [((slot & (1 << n)) != 0,) * 2 for n in range(bits)]
-        for h in range(halves):
-            for lh in range(halves):
-                values = [
-                    x_ref[
-                        order[j], s, (lh * per + k) * D : (lh * per + k + 1) * D,
-                        h * LANES : (h + 1) * LANES,
-                    ]
-                    for k in range(per)
+        blocks = [(h, lh) for h in range(halves) for lh in range(halves)]
+        groups_of = [
+            [
+                x_ref[
+                    order[j], s, (lh * per + k) * D : (lh * per + k + 1) * D,
+                    h * LANES : (h + 1) * LANES,
                 ]
-                values = exchanged(values, masks, D)
-                for d in range(per):
-                    x2_ref[
-                        j, s, (h * per + d) * D : (h * per + d + 1) * D,
-                        lh * LANES : (lh + 1) * LANES,
-                    ] = values[d]
+                for k in range(per)
+            ]
+            for h, lh in blocks
+        ]
+        for (h, lh), values in zip(blocks, exchanged(groups_of, masks, D)):
+            for d in range(per):
+                x2_ref[
+                    j, s, (h * per + d) * D : (h * per + d + 1) * D,
+                    lh * LANES : (lh + 1) * LANES,
+                ] = values[d]
         x2t_ref[j, s] = x2_ref[j, s].T
 
     def cross_layout(s):
@@ -436,12 +441,14 @@
         for n in range(shift):
             bit = (lane >> n) & 1
             masks.append(((bit & (1 - shut)) != 0, (bit | shut) != 0))
-        for h in range(halves):
-            values = [
+        groups_of = [
+            [
                 x_ref[crossing, s, k * D : (k + 1) * D, h * LANES : (h + 1) * LANES]
                 for k in range(D)
             ]
-            values = exchanged(values, masks, 1)
+            for h in range(halves)
+        ]
+        for h, values in enumerate(exchanged(groups_of, masks, 1)):
             for k in range(D):
                 xq_ref[0, s, k * D : (k + 1) * D, h * LANES : (h + 1) * LANES] = values[k]
         xq_ref[1, s] = xq_ref[0, s].T
@@ -524,9 +531,10 @@
         to_down.start()
 
     for s in range(2):
-        for j in range(cols - 1):
+        cross_layout(s)
+    for j in range(cols - 1):
+        for s in range(2):
             relayout(j, s)
-        cross_layout(s)
 
     lefts = [left_first] + majors([outer(i, 1) for i in range(1, cols)])
     rights = minors([outer(i, 3) for i in range(cols - 1)]) + [right_last]
@@ -550,7 +558,7 @@
     def paired(j, kron, left, right, at):
         for s in range(2):
             y = dot(left[j, s], kron_ref[kron]).astype(BF16)
-            gram_ref[at, s] = dot(y, right[j, s])
+            gram_ref[at, s] = dot_nt(y, x2_ref[j, s]) if right is x2t_ref else dot(y, right[j, s])
 
     v_sides = rounded(jnp.where(from_left | from_right, edge_sides, n_sides[0]))
     for j in range(cols - 1):
@@ -567,7 +575,7 @@
         build_kron(kron_ref, final, first, second)
         for s in range(2):
             y = dot(xq_ref[path, s], kron_ref[final]).astype(BF16)
-            gram_ref[final, s] = dot(y, xq_ref[1 - path, s])
+            gram_ref[final, s] = dot_nt(y, xq_ref[path, s])
 
     def all_sides():
         return rounded(joined_sides(side_0, n_sides, [edge_sides])[0])

time: 14.2 us -> 14 us (0.986)
  Pallas kernels: 13.3 us -> 13.1 us
    pallas_call x1, Pallas kernels: 10.6 us -> 10.5 us  [per_device(): pl.pallas_call(functools.partial(messages_kernel, tiles, groups, cols, D)...]
where the time goes in v10:
time: 14 us; the launch traced here: 13.8 us
  Pallas kernels  13.1 us (94%)
  between operations  0.64 us (5%)
    pallas_call x1, Pallas kernels, per_device(): pl.pallas_call(functools.partial(messages_kernel, tiles, groups, cols, D)...  10.5 us
    pallas_call x1, Pallas kernels, per_device(): pl.pallas_call(functools.partial(gates_kernel, tiles, groups, cols, D), o...  2.67 us

profile of v10, /device:TPU:0, one launch (start us, length us, event | category | flops | bytes accessed | tf_op | source)
XLA Modules:
  0.0 13.8 jit_solution(5299891306475931040)
XLA Ops:
  0.6 10.5 %shard_map.41 = (bf16[3,2,256,256]{3,2,1,0:T(8,128)(2,1)S(1)}, f32[2,16,128]{2,1,0:T(8,128)S(1)}, f32[4,16,128]{2,1,0:T(8,128)S(1)}, f32[2,16,128]{2,1,0:T(8,128)S(1)}) custom-call(bf16[3,1024,128]{2,1,0:T(8,128)(2,1)} %bitcast.12, f32[3,4,256]{2,1,0:T(4,128)} %bitcast.13), custom_call_target="tpu_custom_call" | custom-call | tf_op jit(solution)/shard_map/pallas_call | solution.py:899
  11.1 2.7 %shard_map.42 = (bf16[3,1024,128]{2,1,0:T(8,128)(2,1)}, f32[3,4,256]{2,1,0:T(4,128)}) custom-call(bf16[3,2,256,256]{3,2,1,0:T(8,128)(2,1)S(1)} %get-tuple-element.8.ax_ref, f32[2,16,128]{2,1,0:T(8,128)S(1)} %get-tuple-element.9.env_ref, f32[4,16,128]{2,1,0:T(8,128)S(1)} %get-tuple-element.10.inner_ref, f32[2,16,128]{2,1,0:T(8,128)S(1)} %get-tuple-element.11.in_ref), custom_call_target="tpu_custom_call" | custom-call | tf_op jit(solution)/shard_map/pallas_call | solution.py:936

commit v11 on v10

--- a/solution.py
+++ b/solution.py
@@ -10,7 +10,8 @@
 
 ITERS = 2
 NS_STEPS = 6
-EARLY_STEPS = 3
+EARLY_STEPS = 2
+FENCE_STEP = 2
 LANES = 128
 EPSILON = 1e-06
 COUPLING = 0.5
@@ -765,7 +766,7 @@
 
 
 def gates_kernel(tiles, groups, cols, D, ax_ref, env_ref, inner_ref, in_ref, out_hbm, mout_hbm,
-                 kron_ref, out_ref, mout_ref, store_sem):
+                 kron_ref, out_ref, mout_ref, early_ref, fence_ref, store_sem):
     tile = lax.axis_index("tile")
     group = lax.axis_index("group")
     DD = D * D
@@ -786,6 +787,8 @@
         | ((slot == 2 * cols) & (group == 0))
         | ((slot == 2 * cols + 1) & (group == groups - 1))
     )
+    fence = pltpu.make_async_copy(env_ref.at[0], fence_ref, store_sem.at[cols + 1])
+    fence.start()
     state, rotated, trace = bond_open(env_ref[0], env_ref[1])
     begun, turning = inner_ref[0], [inner_ref[1], inner_ref[2]]
     early_left = NS_STEPS - 2 - EARLY_STEPS
@@ -793,10 +796,12 @@
         if step < early_left:
             begun, turning = bond_step(begun, turning)
         elif step == early_left:
-            early = [
-                w.astype(BF16).astype(F32) for w in bond_close(begun, turning, inner_ref[3])
-            ]
+            for s, weight in enumerate(bond_close(begun, turning, inner_ref[3])):
+                early_ref[s] = weight.astype(BF16).astype(F32)
         state, rotated = bond_step(state, rotated)
+        if step == FENCE_STEP:
+            fence.wait()
+    early = [early_ref[s] for s in range(2)]
     late = [
         jnp.where(at_edge, unit, w).astype(BF16).astype(F32)
         for w in bond_close(state, rotated, trace)
@@ -945,7 +950,9 @@
             pltpu.VMEM((4 * cols, DD, DD), BF16),
             pltpu.VMEM(a.shape, BF16),
             pltpu.VMEM((cols, 4, DD), F32),
-            pltpu.SemaphoreType.DMA((cols + 1,)),
+            pltpu.VMEM((2, D, LANES), F32),
+            pltpu.VMEM((D, LANES), F32),
+            pltpu.SemaphoreType.DMA((cols + 2,)),
         ],
         compiler_params=pltpu.CompilerParams(vmem_limit_bytes=24 * 2**20),
     )(gated, env, inner, stacked)

time: 14 us -> 13.9 us (level)
  no operation moved by 1% of the time
where the time goes in v11:
time: 13.9 us; the launch traced here: 13.7 us
  Pallas kernels  13.1 us (94%)
  between operations  0.64 us (5%)
    pallas_call x1, Pallas kernels, per_device(): pl.pallas_call(functools.partial(messages_kernel, tiles, groups, cols, D)...  10.5 us
    pallas_call x1, Pallas kernels, per_device(): pl.pallas_call(functools.partial(gates_kernel, tiles, groups, cols, D), o...  2.6 us

profile of v11, /device:TPU:0, one launch (start us, length us, event | category | flops | bytes accessed | tf_op | source)
XLA Modules:
  0.0 13.7 jit_solution(8740378991871865520)
XLA Ops:
  0.6 10.5 %shard_map.41 = (bf16[3,2,256,256]{3,2,1,0:T(8,128)(2,1)S(1)}, f32[2,16,128]{2,1,0:T(8,128)S(1)}, f32[4,16,128]{2,1,0:T(8,128)S(1)}, f32[2,16,128]{2,1,0:T(8,128)S(1)}) custom-call(bf16[3,1024,128]{2,1,0:T(8,128)(2,1)} %bitcast.12, f32[3,4,256]{2,1,0:T(4,128)} %bitcast.13), custom_call_target="tpu_custom_call" | custom-call | tf_op jit(solution)/shard_map/pallas_call | solution.py:904
  11.1 2.6 %shard_map.42 = (bf16[3,1024,128]{2,1,0:T(8,128)(2,1)}, f32[3,4,256]{2,1,0:T(4,128)}) custom-call(bf16[3,2,256,256]{3,2,1,0:T(8,128)(2,1)S(1)} %get-tuple-element.8.ax_ref, f32[2,16,128]{2,1,0:T(8,128)S(1)} %get-tuple-element.9.env_ref, f32[4,16,128]{2,1,0:T(8,128)S(1)} %get-tuple-element.10.inner_ref, f32[2,16,128]{2,1,0:T(8,128)S(1)} %get-tuple-element.11.in_ref), custom_call_target="tpu_custom_call" | custom-call | tf_op jit(solution)/shard_map/pallas_call | solution.py:941

commit v12 on v11

--- a/solution.py
+++ b/solution.py
@@ -313,7 +313,7 @@
 
         @pl.when(jnp.logical_not(has_up))
         def _():
-            dst[...] = edges
+            dst[...] = edges.astype(BF16)
 
     def below_arrives(sent, arriving, dst, edges):
         @pl.when(has_down)
@@ -323,7 +323,7 @@
 
         @pl.when(jnp.logical_not(has_down))
         def _():
-            dst[...] = edges
+            dst[...] = edges.astype(BF16)
 
     def joined_rows(above, below):
         return [
@@ -335,7 +335,7 @@
     from_right = (slot == 2 * cols - 1) | (slot == 2 * cols + 1)
 
     def joined_sides(dst, local, edges):
-        got = dst[...]
+        got = dst[...].astype(F32)
         out = []
         for k, (value, edge) in enumerate(zip(local, edges)):
             other = got[k * D : (k + 1) * D]
@@ -495,7 +495,8 @@
     for i in range(cols - 1):
         first_gram(1, i)
     (left_first,), (right_last,) = majors([outer(0, 1)]), minors([outer(cols - 1, 3)])
-    send_s0[...] = normalised([jnp.where(from_left, right_last[0], left_first[0])])[0]
+    (side_out,) = normalised([jnp.where(from_left, right_last[0], left_first[0])])
+    send_s0[...] = side_out.astype(BF16)
     ups = [outer(i, 0) for i in range(cols)]
 
     mix = jnp.full((D, DD), math.tanh(FIELD), BF16)
@@ -519,7 +520,7 @@
     sides_0.start()
     downs = majors([outer(i, 2) for i in range(cols)])
     ups = minors(ups)
-    send_v0[...] = normalised([upright(downs, ups, 0)])[0]
+    send_v0[...] = normalised([upright(downs, ups, 0)])[0].astype(BF16)
     to_up = copy(send_v0, down_0, 0, 0, {"tile": tile - 1})
     to_down = copy(send_v0, up_0, 0, 1, {"tile": tile + 1})
 
@@ -589,7 +590,7 @@
 
     def ship(buffer, values):
         for k in range(2):
-            buffer[k * D : (k + 1) * D] = values[k]
+            buffer[k * D : (k + 1) * D] = values[k].astype(BF16)
 
     def ordered(above, below, kind):
         return placed(
@@ -614,7 +615,7 @@
     @pl.when(far_up)
     def _():
         below_0()
-        near = rounded(down_0[...])
+        near = down_0[...].astype(F32)
         crossing_gram(by_major(near, cols + crossing), other_minor, 0)
         early = [up_legs(by_major(near, cols + order[j]), j) for j in range(cols - 1)]
         early = minors(early)
@@ -628,7 +629,7 @@
             up_far.start()
 
         above_0()
-        weight = by_minor(rounded(up_0[...]), crossing)
+        weight = by_minor(up_0[...].astype(F32), crossing)
         (cross,) = majors([cross_minor(final, weight)])
         ship(send_s1, normalised(cross))
         sides_1.start()
@@ -636,7 +637,7 @@
     @pl.when(far_down)
     def _():
         above_0()
-        near = rounded(up_0[...])
+        near = up_0[...].astype(F32)
         crossing_gram(other_major, by_minor(near, crossing), 1)
         early = [down_legs(by_minor(near, order[j]), j) for j in range(cols - 1)]
         early = majors(early)
@@ -650,12 +651,12 @@
             down_far.start()
 
         below_0()
-        weight = by_major(rounded(down_0[...]), cols + crossing)
+        weight = by_major(down_0[...].astype(F32), cols + crossing)
         (cross,) = minors([cross_major(final, weight)])
         ship(send_s1, normalised(cross))
         sides_1.start()
 
-    v_rows = rounded(joined_rows(up_0[...], down_0[...])[0])
+    v_rows = rounded(joined_rows(up_0[...].astype(F32), down_0[...].astype(F32))[0])
     weights = []
     for j in range(cols):
         i = order[j]
@@ -716,7 +717,10 @@
         slot < cols, lane + half, jnp.where(slot < 2 * cols, lane - half, lane)
     )
     o_rows = [
-        pick(send_f1[k * D : (k + 1) * D] + send_v1[k * D : (k + 1) * D], swapped)
+        pick(
+            send_f1[k * D : (k + 1) * D].astype(F32) + send_v1[k * D : (k + 1) * D].astype(F32),
+            swapped,
+        )
         for k in range(2)
     ]
     others = [horizontal(j) for j in range(cols - 1)]
@@ -741,7 +745,7 @@
 
     is_cross = (slot == cross_slot) | (slot == jnp.where(group == 0, 2 * cols + 1, 2 * cols))
     o_sides = [
-        jnp.where(is_cross, send_s1[k * D : (k + 1) * D], value)
+        jnp.where(is_cross, send_s1[k * D : (k + 1) * D].astype(F32), value)
         for k, value in enumerate(normalised([own_sides(k) for k in range(2)]))
     ]
     n_sides = normalised([other_sides(k) for k in range(2)])
@@ -756,7 +760,11 @@
     rows_edges = jnp.concatenate([edge_rows, zero], axis=0)
     above_arrives(up_near, down_near, up_1, rows_edges)
     below_arrives(down_near, up_near, down_1, rows_edges)
-    n_rows = joined_rows(up_1[...], down_1[...])
+    n_rows = joined_rows(up_1[...].astype(F32), down_1[...].astype(F32))
+    on_edge = ((slot < cols) & jnp.logical_not(has_up)) | (
+        (slot >= cols) & (slot < 2 * cols) & jnp.logical_not(has_down)
+    )
+    n_rows[0] = jnp.where(on_edge, edge_rows, n_rows[0])
     for k in range(2):
         env_ref[k] = jnp.where(
             slot < 2 * cols, o_rows[k] + n_rows[k], o_sides[k] + n_sides[k]
@@ -924,7 +932,7 @@
             pltpu.VMEM((2 * cols, 2, DD, DD), F32),
         ]
         + [
-            pltpu.VMEM(((1 + turn) * D, LANES), F32) for _ in range(6) for turn in range(ITERS)
+            pltpu.VMEM(((1 + turn) * D, LANES), BF16) for _ in range(6) for turn in range(ITERS)
         ]
         + [
             pltpu.SemaphoreType.DMA((ITERS, 3)),

time: 13.9 us -> 13.8 us (level)
  Pallas kernels: 13.1 us -> 12.9 us
    pallas_call x1, Pallas kernels: 10.5 us -> 10.3 us  [per_device(): pl.pallas_call(functools.partial(messages_kernel, tiles, groups, cols, D)...]
where the time goes in v12:
time: 13.8 us; the launch traced here: 13.5 us
  Pallas kernels  12.9 us (93%)
  between operations  0.64 us (5%)
    pallas_call x1, Pallas kernels, per_device(): pl.pallas_call(functools.partial(messages_kernel, tiles, groups, cols, D)...  10.3 us
    pallas_call x1, Pallas kernels, per_device(): pl.pallas_call(functools.partial(gates_kernel, tiles, groups, cols, D), o...  2.6 us

profile of v12, /device:TPU:0, one launch (start us, length us, event | category | flops | bytes accessed | tf_op | source)
XLA Modules:
  0.0 13.5 jit_solution(6355471201747025970)
XLA Ops:
  0.6 10.3 %shard_map.41 = (bf16[3,2,256,256]{3,2,1,0:T(8,128)(2,1)S(1)}, f32[2,16,128]{2,1,0:T(8,128)S(1)}, f32[4,16,128]{2,1,0:T(8,128)S(1)}, f32[2,16,128]{2,1,0:T(8,128)S(1)}) custom-call(bf16[3,1024,128]{2,1,0:T(8,128)(2,1)} %bitcast.12, f32[3,4,256]{2,1,0:T(4,128)} %bitcast.13), custom_call_target="tpu_custom_call" | custom-call | tf_op jit(solution)/shard_map/pallas_call | solution.py:912
  10.9 2.6 %shard_map.42 = (bf16[3,1024,128]{2,1,0:T(8,128)(2,1)}, f32[3,4,256]{2,1,0:T(4,128)}) custom-call(bf16[3,2,256,256]{3,2,1,0:T(8,128)(2,1)S(1)} %get-tuple-element.8.ax_ref, f32[2,16,128]{2,1,0:T(8,128)S(1)} %get-tuple-element.9.env_ref, f32[4,16,128]{2,1,0:T(8,128)S(1)} %get-tuple-element.10.inner_ref, f32[2,16,128]{2,1,0:T(8,128)S(1)} %get-tuple-element.11.in_ref), custom_call_target="tpu_custom_call" | custom-call | tf_op jit(solution)/shard_map/pallas_call | solution.py:949
